TPU v7x, 256 devices: a whole 4x4x8 slice. The times are simulated.
256 devices in a mesh: gx: 16 (over y, x), gy: 16 (over z, core).
Axes of the slice: x: 4, y: 4, z: 8, core: 2. Of those that a mesh axis runs over, the one named last changes fastest.
Arguments:
- spatial_factor: float32 [64, 256, 32, 64], P('gx', 'gy'), may hold values from -60 to 60
- coupling: float32 [64, 64], replicated, may hold values from -1 to 5
- orient_factor: float32 [2048, 64], replicated, may hold values from -6 to 6
- directions: float32 [3, 2048], replicated, may hold values from -1 to 1, as said below
Outputs:
- new_spatial: float32 [64, 256, 32, 64], P('gx', 'gy')
- new_coupling: float32 [64, 64], replicated
- new_orient: float32 [2048, 64], replicated
Inputs may be any that keep to these rules, and one draw needn't show every extreme that they name: `directions`: each column is a unit vector.
All inputs are finite; a program needn't handle non-finite values.
Results may differ from a plain program's by a relative error of at most 0.0003.
Values sent between devices are 32-bit elements; how exact they have to be, the bound alone decides.
A program may use at most 64 MiB of HBM per device.

v0:
```python
import functools

import jax
import jax.numpy as jnp
from jax import lax
from jax.experimental import pallas as pl
from jax.experimental.pallas import tpu as pltpu
from jax.sharding import PartitionSpec as P

STEPS = 2
MESH = pl.DeviceIdType.MESH
F32 = jnp.float32
BF16 = jnp.bfloat16
NN = (((1,), (0,)), ((), ()))
NT = (((1,), (1,)), ((), ()))

courant = 0.3
tumble = 0.2


def mm(a, b, dims=NN):
    return lax.dot_general(a, b, dims, precision=lax.Precision.HIGHEST, preferred_element_type=F32)


def bdot(a, b, dims=NN):
    return lax.dot_general(a, b, dims, preferred_element_type=F32)


def split(a):
    hi = a.astype(BF16)
    return hi, (a - hi.astype(F32)).astype(BF16)


def left3(a):
    hi, lo = split(a)
    return jnp.concatenate([hi, hi, lo], axis=1)


def right3(b):
    hi, lo = split(b)
    return jnp.concatenate([hi, lo, hi], axis=0)


def gram3(left_hi, left_lo, right_hi, right_lo):
    width = right_hi.shape[0]
    first = bdot(left_hi, jnp.concatenate([right_hi, right_lo], axis=0), NT)
    return first[:, :width] + first[:, width:] + bdot(left_lo, right_hi, NT)


def speed_of(density):
    return 1.0 / (1.0 + density * density)


def eliminate(gram):
    n = gram.shape[0]
    rows = lax.broadcasted_iota(jnp.int32, (8, 2 * n), 0)
    lanes = lax.broadcasted_iota(jnp.int32, (n, n), 1)
    eye = jnp.where(lax.broadcasted_iota(jnp.int32, (n, n), 0) == lanes, 1.0, 0.0)
    both = jnp.concatenate([gram, eye], axis=1)
    blocks = [both[8 * b : 8 * b + 8] for b in range(n // 8)]
    for k in range(n):
        kb, ks = divmod(k, 8)
        pivot = blocks[kb][ks : ks + 1, k : k + 1]
        inverse = 1.0 / pivot
        row = blocks[kb][ks : ks + 1, :]
        scaled = row * inverse
        for b in range(kb, n // 8):
            factor = blocks[b][:, k : k + 1]
            update = blocks[b] - factor * scaled
            if b == kb:
                blocks[b] = jnp.where(rows > ks, update, blocks[b])
            else:
                blocks[b] = update
    whole = jnp.concatenate(blocks, axis=0)
    diagonal = jnp.sum(whole[:, :n] * eye, axis=1, keepdims=True)
    whole = whole / jnp.sqrt(diagonal)
    upper = jnp.where(lanes >= lax.broadcasted_iota(jnp.int32, (n, n), 0), whole[:, :n], 0.0)
    return upper, whole[:, n:]


def kernel(
    sizes, x_ref, s_ref, v_ref, d_ref, x_out, s_out, v_out,
    k_s, base_s, tpx_s, tmx_s, t_s, k1_s, h_s, khx_s, khy_s, hhy_s, v_s, yface_s,
    xhalo_s, yhalo_s, pay_s, r1_s, c_s, r2_s, f_s, r3_s,
    hsend, hrecv, asend, arecv,
):
    ngx, ngy, slabs, ylen, zlen = sizes
    slab = ylen * zlen
    nloc = slabs * slab
    chunks = slab // 128
    cells = float(nloc * ngx * ngy)
    no = v_ref.shape[0]
    rank = 64
    c, t = courant, tumble
    me_x, me_y = lax.axis_index("gx"), lax.axis_index("gy")
    crow = 256 // ngy

    barrier = pltpu.get_barrier_semaphore()

    def greet_x(i, _):
        pl.semaphore_signal(barrier, inc=1, device_id={"gx": lax.rem(me_x + i, ngx), "gy": me_y}, device_id_type=MESH)
        return 0

    def greet_y(i, _):
        pl.semaphore_signal(barrier, inc=1, device_id={"gx": me_x, "gy": lax.rem(me_y + i, ngy)}, device_id_type=MESH)
        return 0

    lax.fori_loop(1, ngx, greet_x, 0)
    lax.fori_loop(1, ngy, greet_y, 0)

    eye = jnp.where(
        lax.broadcasted_iota(jnp.int32, (rank, rank), 0) == lax.broadcasted_iota(jnp.int32, (rank, rank), 1), 1.0, 0.0
    )
    lane = lax.broadcasted_iota(jnp.int32, (rank, 128), 1)
    zpos = lax.rem(lane, zlen)
    group = lane // zlen
    per = 128 // zlen

    def cut(a):
        return [a[:, 128 * i : 128 * i + 128] for i in range(a.shape[1] // 128)]

    def roll(a, s):
        s = s % 128
        return a if s == 0 else pltpu.roll(a, s, 1)

    def from_y_before(a, halo, q):
        rolled = [roll(piece, zlen) for piece in cut(a)]
        last = roll(halo, zlen * (-q))
        out = []
        for piece in rolled:
            out.append(jnp.where(lane < zlen, last, piece))
            last = piece
        return jnp.concatenate(out, axis=1)

    def from_y_after(a, halo, q):
        rolled = [roll(piece, -zlen) for piece in cut(a)] + [roll(halo, 128 - zlen - zlen * q)]
        return jnp.concatenate(
            [jnp.where(lane < 128 - zlen, rolled[i], rolled[i + 1]) for i in range(len(rolled) - 1)], axis=1
        )

    def from_z_before(a):
        return jnp.concatenate([jnp.where(zpos == 0, roll(p, 1 - zlen), roll(p, 1)) for p in cut(a)], axis=1)

    def from_z_after(a):
        return jnp.concatenate([jnp.where(zpos == zlen - 1, roll(p, zlen - 1), roll(p, -1)) for p in cut(a)], axis=1)

    def faces(ref):
        first, last = jnp.zeros((rank, 128), F32), jnp.zeros((rank, 128), F32)
        for q in range(slabs):
            low = ref[:, slab * q : slab * q + 128]
            high = ref[:, slab * q + slab - 128 : slab * q + slab]
            first = jnp.where(group == q, roll(low, zlen * q), first)
            last = jnp.where(group == q, roll(high, zlen * q - (128 - zlen)), last)
        return first, last

    def halo_copies(ref, e):
        left = {"gx": lax.rem(me_x + ngx - 1, ngx), "gy": me_y}
        right = {"gx": lax.rem(me_x + 1, ngx), "gy": me_y}
        below = {"gx": me_x, "gy": lax.rem(me_y + ngy - 1, ngy)}
        above = {"gx": me_x, "gy": lax.rem(me_y + 1, ngy)}
        plan = [
            (ref.at[:, pl.ds(nloc - slab, slab)], xhalo_s.at[e, 0], right),
            (ref.at[:, pl.ds(0, slab)], xhalo_s.at[e, 1], left),
            (yface_s.at[e, 1], yhalo_s.at[e, 0], above),
            (yface_s.at[e, 0], yhalo_s.at[e, 1], below),
        ]
        return [
            pltpu.make_async_remote_copy(
                src_ref=src, dst_ref=dst, send_sem=hsend.at[e, i], recv_sem=hrecv.at[e, i], device_id=to, device_id_type=MESH
            )
            for i, (src, dst, to) in enumerate(plan)
        ]

    def spread(phase, step, src_of, dst, mine, n, axis):
        def copy(i):
            to = lax.rem(mine + i, n)
            ids = {"gx": to, "gy": me_y} if axis == "gx" else {"gx": me_x, "gy": to}
            return pltpu.make_async_remote_copy(
                src_ref=src_of(to), dst_ref=dst.at[step, mine], send_sem=asend.at[step, phase, i],
                recv_sem=arecv.at[step, phase, mine], device_id=ids, device_id_type=MESH,
            )

        def start(i, _):
            copy(i).start()
            return 0

        lax.fori_loop(1, n, start, 0)

    def settle(phase, step, src_of, dst, mine, n, axis):
        def wait(i, _):
            source = lax.rem(mine + i, n)
            ids = {"gx": source, "gy": me_y} if axis == "gx" else {"gx": me_x, "gy": source}
            arrived = pltpu.make_async_remote_copy(
                src_ref=src_of(source), dst_ref=dst.at[step, source], send_sem=asend.at[step, phase, i],
                recv_sem=arecv.at[step, phase, source], device_id=ids, device_id_type=MESH,
            )
            arrived.wait_recv()
            arrived.wait_send()
            return 0

        lax.fori_loop(1, n, wait, 0)

    st = left3(mm(eye, s_ref[...], NT))
    for q in range(slabs):
        x_hi, x_lo = split(x_ref[slab * q : slab * q + slab, :])
        k_s[:, slab * q : slab * q + slab] = (
            bdot(st[:, :rank], x_hi, NT) + bdot(st[:, rank : 2 * rank], x_lo, NT) + bdot(st[:, 2 * rank :], x_hi, NT)
        )
    first, last = faces(k_s)
    yface_s[0, 0] = first
    yface_s[0, 1] = last
    pl.semaphore_wait(barrier, ngx + ngy - 2)
    first_halo = halo_copies(k_s, 0)
    for copy in first_halo:
        copy.start()
    for i in range(no // 512):
        v_s[:, 512 * i : 512 * i + 512] = mm(eye, v_ref[512 * i : 512 * i + 512, :], NT)

    def step_body(step):
        total = jnp.zeros((6 * rank + 16, rank), F32)
        for i in range(no // 512):
            v = v_s[:, 512 * i : 512 * i + 512]
            v_hi, v_lo = split(v)
            d = d_ref[:, 512 * i : 512 * i + 512]
            parts = []
            for dim in range(3):
                parts.append(v * jnp.maximum(d[dim : dim + 1], 0.0))
            for dim in range(3):
                parts.append(v * jnp.maximum(-d[dim : dim + 1], 0.0))
            parts.append(jnp.ones((16, 512), F32))
            l_hi, l_lo = split(jnp.concatenate(parts, axis=0))
            total = total + gram3(l_hi, l_lo, v_hi, v_lo)
        total = total * (1.0 / no)
        tables = [total[rank * i : rank * i + rank] for i in range(6)]
        u_row = total[6 * rank : 6 * rank + 1]
        u_col = jnp.sum(eye * u_row, axis=1, keepdims=True)
        center = tables[0] + tables[1] + tables[2] + tables[3] + tables[4] + tables[5]
        stencil = left3(c * jnp.concatenate([center] + tables, axis=0))

        if step == 0:
            for copy in first_halo:
                copy.wait()
            for i in range(2):
                khx_s[i] = xhalo_s[0, i]
                khy_s[i] = yhalo_s[0, i]

        def flux(k):
            density = jnp.sum(k * u_col, axis=0, keepdims=True)
            return density, speed_of(density) * k

        for q in range(slabs):
            k = k_s[:, slab * q : slab * q + slab]
            density, g = flux(k)
            out = bdot(stencil, right3(g))
            base_s[:, slab * q : slab * q + slab] = (1.0 - t) * k + t * u_col * density - out[:rank]
            tpx_s[:, slab * (q + 1) : slab * (q + 2)] = out[rank : 2 * rank]
            tmx_s[:, slab * q : slab * (q + 1)] = out[4 * rank : 5 * rank]
            t_s[0, :, slab * q : slab * q + slab] = out[2 * rank : 3 * rank]
            t_s[1, :, slab * q : slab * q + slab] = out[5 * rank : 6 * rank]
            t_s[2, :, slab * q : slab * q + slab] = out[3 * rank : 4 * rank]
            t_s[3, :, slab * q : slab * q + slab] = out[6 * rank : 7 * rank]
        tpx_s[:, :slab] = bdot(stencil[rank : 2 * rank], right3(flux(khx_s[0])[1]))
        tmx_s[:, slab * slabs :] = bdot(stencil[4 * rank : 5 * rank], right3(flux(khx_s[1])[1]))
        tpy = bdot(stencil[2 * rank : 3 * rank], right3(flux(khy_s[0])[1]))
        tmy = bdot(stencil[5 * rank : 6 * rank], right3(flux(khy_s[1])[1]))
        for q in range(slabs):
            here = slice(slab * q, slab * q + slab)
            k1_s[:, here] = (
                base_s[:, here]
                + tpx_s[:, here]
                + tmx_s[:, slab * (q + 1) : slab * (q + 2)]
                + from_y_before(t_s[0, :, here], tpy, q)
                + from_y_after(t_s[1, :, here], tmy, q)
                + from_z_before(t_s[2, :, here])
                + from_z_after(t_s[3, :, here])
            )
        first, last = faces(k1_s)
        yface_s[step + 1, 0] = first
        yface_s[step + 1, 1] = last
        halo = halo_copies(k1_s, step + 1)
        for copy in halo:
            copy.start()

        for q in range(slabs):
            h_s[:, slab * (q + 1) : slab * (q + 2)] = flux(k1_s[:, slab * q : slab * q + slab])[1]
        for copy in halo:
            copy.wait()
        h_s[:, :slab] = flux(xhalo_s[step + 1, 0])[1]
        h_s[:, slab * (slabs + 1) :] = flux(xhalo_s[step + 1, 1])[1]
        hy = [flux(yhalo_s[step + 1, i])[1] for i in range(2)]
        raw = jnp.zeros((7 * rank, rank), F32)
        for q in range(slabs):
            k1 = k1_s[:, slab * q : slab * q + slab]
            h = h_s[:, slab * (q + 1) : slab * (q + 2)]
            stack = jnp.concatenate(
                [
                    k1,
                    h - h_s[:, slab * q : slab * (q + 1)],
                    h - from_y_before(h, hy[0], q),
                    h - from_z_before(h),
                    h_s[:, slab * (q + 2) : slab * (q + 3)] - h,
                    from_y_after(h, hy[1], q) - h,
                    from_z_after(h) - h,
                ],
                axis=0,
            )
            l_hi, l_lo = split(stack)
            raw = raw + gram3(l_hi, l_lo, l_hi[:rank], l_lo[:rank])
        packed = jnp.concatenate(
            [raw[: 4 * rank], jnp.concatenate([raw[4 * rank :], jnp.zeros((rank, rank), F32)], axis=0)], axis=1
        )
        pay_s[step] = packed.reshape(ngy, crow, 128)

        chunk = lambda j: pay_s.at[step, j]
        spread(0, step, chunk, r1_s, me_y, ngy, "gy")
        r1_s[step, me_y] = pay_s[step, me_y]
        settle(0, step, chunk, r1_s, me_y, ngy, "gy")
        c_s[step] = jnp.sum(r1_s[step], axis=0)
        own = lambda j: c_s.at[step]
        spread(1, step, own, r2_s, me_x, ngx, "gx")
        r2_s[step, me_x] = c_s[step]
        settle(1, step, own, r2_s, me_x, ngx, "gx")
        f_s[step] = jnp.sum(r2_s[step], axis=0)
        summed = lambda j: f_s.at[step]
        spread(2, step, summed, r3_s, me_y, ngy, "gy")
        r3_s[step, me_y] = f_s[step]
        settle(2, step, summed, r3_s, me_y, ngy, "gy")
        full = r3_s[step].reshape(256, 128) * (1.0 / cells)

        upper, inverse = eliminate(full[:rank, :rank])
        z_stack = jnp.concatenate([full[rank:, :rank], full[: 3 * rank, rank:]], axis=0)
        q_wide = mm(inverse, z_stack, NT)
        q_stack = jnp.concatenate([q_wide[:, rank * i : rank * i + rank] for i in range(6)], axis=0)
        m_stack = mm(q_stack, inverse, NT)
        ms = mm(m_stack, upper)
        su = jnp.sum(upper * u_row, axis=1, keepdims=True)
        s2 = (1.0 + t) * upper - t * (su * u_row)
        for dim in range(3):
            s2 = s2 + c * mm(ms[rank * dim : rank * dim + rank], tables[dim])
            s2 = s2 - c * mm(ms[rank * (dim + 3) : rank * (dim + 4)], tables[dim + 3])
        mean = jnp.sum(s2 * u_row, axis=1, keepdims=True)
        left = left3(jnp.concatenate([s2, c * mm(m_stack, s2)], axis=0))
        gram = jnp.zeros((rank, rank), F32)
        for i in range(no // 512):
            here = slice(512 * i, 512 * i + 512)
            out = bdot(left, right3(v_s[:, here]))
            d = d_ref[:, here]
            l1 = (1.0 - t) * out[:rank] + t * mean
            for dim in range(3):
                l1 = l1 - jnp.maximum(d[dim : dim + 1], 0.0) * out[rank * (dim + 1) : rank * (dim + 2)]
                l1 = l1 + jnp.maximum(-d[dim : dim + 1], 0.0) * out[rank * (dim + 4) : rank * (dim + 5)]
            v_s[:, here] = l1
            hi, lo = split(l1)
            gram = gram + gram3(hi, lo, hi, lo)
        v_upper, v_inverse = eliminate(gram * (1.0 / no))
        vi = left3(v_inverse)
        last_step = step == STEPS - 1
        for i in range(no // 512):
            here = slice(512 * i, 512 * i + 512)
            v = bdot(vi, right3(v_s[:, here]))
            if last_step:
                v_out[here, :] = jnp.concatenate([v, v], axis=0).T[:, :rank]
            else:
                v_s[:, here] = v
        if last_step:
            s_out[...] = mm(eye, v_upper, NT)
            wt = left3(inverse)
        else:
            wt = left3(mm(v_upper, inverse))
        for q in range(slabs):
            here = slice(slab * q, slab * q + slab)
            k = bdot(wt, right3(k1_s[:, here]))
            if last_step:
                x_out[here, :] = jnp.concatenate([k, k], axis=0).T[:, :rank]
            else:
                k_s[:, here] = k
        if not last_step:
            for i in range(2):
                khx_s[i] = bdot(wt, right3(xhalo_s[step + 1, i]))
                khy_s[i] = bdot(wt, right3(yhalo_s[step + 1, i]))

    for step in range(STEPS):
        step_body(step)


def solution(mesh):
    ngx, ngy = mesh.shape["gx"], mesh.shape["gy"]

    def shards(spatial, coupling, orient, directions):
        slabs, ylen, zlen, rank = spatial.shape
        slab = ylen * zlen
        nloc = slabs * slab
        no = orient.shape[0]
        crow = 256 // ngy
        vmem = pl.BlockSpec(memory_space=pltpu.VMEM)
        scratch = [
            (rank, nloc), (rank, nloc), (rank, nloc + slab), (rank, nloc + slab), (4, rank, nloc), (rank, nloc),
            (rank, nloc + 2 * slab), (2, rank, slab), (2, rank, 128), (2, rank, 128), (rank, no),
            (STEPS + 1, 2, rank, 128), (STEPS + 1, 2, rank, slab), (STEPS + 1, 2, rank, 128),
            (STEPS, ngy, crow, 128), (STEPS, ngy, crow, 128), (STEPS, crow, 128), (STEPS, ngx, crow, 128),
            (STEPS, crow, 128), (STEPS, ngy, crow, 128),
        ]
        n = max(ngx, ngy)
        x, s, v = pl.pallas_call(
            functools.partial(kernel, (ngx, ngy, slabs, ylen, zlen)),
            out_shape=(
                jax.ShapeDtypeStruct((nloc, rank), F32),
                jax.ShapeDtypeStruct((rank, rank), F32),
                jax.ShapeDtypeStruct((no, rank), F32),
            ),
            in_specs=[vmem] * 4,
            out_specs=(vmem, vmem, vmem),
            scratch_shapes=[pltpu.VMEM(shape, F32) for shape in scratch]
            + [
                pltpu.SemaphoreType.DMA((STEPS + 1, 4)),
                pltpu.SemaphoreType.DMA((STEPS + 1, 4)),
                pltpu.SemaphoreType.DMA((STEPS, 3, n)),
                pltpu.SemaphoreType.DMA((STEPS, 3, n)),
            ],
            compiler_params=pltpu.CompilerParams(
                collective_id=0, has_side_effects=True, vmem_limit_bytes=60 * 1024 * 1024
            ),
        )(spatial.reshape(nloc, rank), coupling, orient, directions)
        return x.reshape(spatial.shape), s, v

    return jax.shard_map(
        shards,
        mesh=mesh,
        in_specs=(P("gx", "gy", None, None), P(), P(), P()),
        out_specs=(P("gx", "gy", None, None), P(), P()),
        check_vma=False,
    )
```

profile of v0, /device:TPU:1, one launch (start us, length us, event | category | flops | bytes accessed | tf_op | source)
XLA Modules:
  0.0 110.7 jit_solution(11641705640170165533)
XLA Ops:
  0.6 2.4 %copy.7.v_ref = f32[2048,64]{1,0:T(8,128)} copy(f32[2048,64]{0,1:T(8,128)} %param.6) | data formatting | bytes 1048576 | tf_op args[2]
  3.0 103.7 %shard_map.67 = (f32[2048,64]{1,0:T(8,128)}, f32[64,64]{1,0:T(8,128)}, f32[2048,64]{1,0:T(8,128)}) custom-call(f32[2048,64]{1,0:T(8,128)} %bitcast.2, f32[64,64]{1,0:T(8,128)} %s_ref.1, f32[2048,64]{1,0:T(8,128)} %copy.7.v_ref, f32[3,2048]{1,0:T(4,128)} %d_ref.1), custom_call_target="tpu_custom_call" | custom-call | tf_op jit(solution)/shard_map/pallas_call | solution.py:404
  106.7 0.0 copy-start
  106.7 2.4 %copy.8 = f32[2048,64]{0,1:T(8,128)} copy(f32[2048,64]{1,0:T(8,128)} %get-tuple-element.11) | data formatting | bytes 1048576
  109.1 0.0 copy-done
  109.1 0.0 copy-start.1
  109.1 1.0 copy.11
  110.1 0.0 copy-done.1
  110.1 0.6 copy.12
Async XLA Ops:
  106.7 2.4 %copy-start = (f32[2048,64]{1,0:T(8,128)S(1)}, f32[2048,64]{1,0:T(8,128)}, u32[]{:S(2)}) copy-start(f32[2048,64]{1,0:T(8,128)} %get-tuple-element.6) | copy-start | bytes 1572868
  109.1 1.0 copy-start.1
where the time goes:
time: 111 us
  Pallas kernels  104 us (94%)
  local copies, waits for them, and re-layouts  6.37 us (6%)
    pallas_call x1, Pallas kernels, shards(): pl.pallas_call(functools.partial(kernel, (ngx, ngy, slabs, ylen, zlen)),...  104 us
    unnamed x8, local copies, waits for them, and re-layouts  6.37 us

commit v1 on v0

v1 whole, which is shorter than its diff:
```python
import functools

import jax
import jax.numpy as jnp
from jax import lax
from jax.experimental import pallas as pl
from jax.experimental.pallas import tpu as pltpu
from jax.sharding import PartitionSpec as P

STEPS = 2
MESH = pl.DeviceIdType.MESH
F32 = jnp.float32
BF16 = jnp.bfloat16
NN = (((1,), (0,)), ((), ()))
NT = (((1,), (1,)), ((), ()))

courant = 0.3
tumble = 0.2


def mm(a, b, dims=NN):
    return lax.dot_general(a, b, dims, precision=lax.Precision.HIGHEST, preferred_element_type=F32)


def bdot(a, b, dims=NN):
    return lax.dot_general(a, b, dims, preferred_element_type=F32)


def split(a):
    hi = a.astype(BF16)
    return hi, (a - hi.astype(F32)).astype(BF16)


def left3(a):
    hi, lo = split(a)
    return jnp.concatenate([hi, hi, lo], axis=1)


def right3(b):
    hi, lo = split(b)
    return jnp.concatenate([hi, lo, hi], axis=0)


def gram3(left_hi, left_lo, right_hi, right_lo):
    width = right_hi.shape[0]
    first = bdot(left_hi, jnp.concatenate([right_hi, right_lo], axis=0), NT)
    return first[:, :width] + first[:, width:] + bdot(left_lo, right_hi, NT)


def speed_of(density):
    return 1.0 / (1.0 + density * density)


def begin(gram):
    n = gram.shape[0]
    eye = jnp.where(lax.broadcasted_iota(jnp.int32, (n, n), 0) == lax.broadcasted_iota(jnp.int32, (n, n), 1), 1.0, 0.0)
    both = jnp.concatenate([gram, eye], axis=1)
    return [both[8 * b : 8 * b + 8] for b in range(n // 8)]


def advance(blocks, start, stop):
    width = blocks[0].shape[1]
    below = lax.broadcasted_iota(jnp.int32, (8, width), 0)

    def across(a, c):
        return jnp.broadcast_to(a[:, c : c + 1], (8, width))

    def down(a, r):
        return jnp.broadcast_to(a[r : r + 1], (8, width))

    for kb in range(start, stop):
        own = [across(blocks[kb], 8 * kb + c) for c in range(8)]
        rows, inverses, heads = [], [], []
        current = blocks[kb]
        for k in range(8):
            head = {j: down(own[j], k) for j in range(k, 8)}
            inverse = 1.0 / head[k]
            row = down(current, k)
            factor = jnp.where(below > k, own[k] * inverse, 0.0)
            for j in range(k + 1, 8):
                own[j] = own[j] - factor * head[j]
            current = current - factor * row
            rows.append(row)
            inverses.append(inverse)
            heads.append(head)
        blocks[kb] = current
        for b in range(kb + 1, len(blocks)):
            columns = [across(blocks[b], 8 * kb + c) for c in range(8)]
            for k in range(8):
                factor = columns[k] * inverses[k]
                for j in range(k + 1, 8):
                    columns[j] = columns[j] - factor * heads[k][j]
                blocks[b] = blocks[b] - factor * rows[k]
    return blocks


def finish(blocks):
    whole = jnp.concatenate(blocks, axis=0)
    n = whole.shape[0]
    i, j = (lax.broadcasted_iota(jnp.int32, (n, n), d) for d in range(2))
    diagonal = jnp.sum(jnp.where(i == j, whole[:, :n], 0.0), axis=1, keepdims=True)
    whole = whole * (1.0 / jnp.sqrt(diagonal))
    return jnp.where(j >= i, whole[:, :n], 0.0), whole[:, n:]


def kernel(
    sizes, x_ref, s_ref, v_ref, d_ref, x_out, s_out, v_out,
    k_s, base_s, tpx_s, tmx_s, t_s, k1_s, h_s, khx_s, khy_s, v_s, yface_s,
    xhalo_s, yhalo_s, pay_s, r1_s, c_s, r2_s, f_s, r3_s, den_s, g3_s, kk_s,
    hsend, hrecv, asend, arecv,
):
    ngx, ngy, slabs, ylen, zlen = sizes
    slab = ylen * zlen
    nloc = slabs * slab
    cells = float(nloc * ngx * ngy)
    no = v_ref.shape[1]
    rank = 64
    c, t = courant, tumble
    me_x, me_y = lax.axis_index("gx"), lax.axis_index("gy")
    crow = 128 // ngy
    signs = ((0, 1), (1, 1), (0, -1), (1, -1), (2, 1), (2, -1))

    barrier = pltpu.get_barrier_semaphore()

    def greet_x(i, _):
        pl.semaphore_signal(barrier, inc=1, device_id={"gx": lax.rem(me_x + i, ngx), "gy": me_y}, device_id_type=MESH)
        return 0

    def greet_y(i, _):
        pl.semaphore_signal(barrier, inc=1, device_id={"gx": me_x, "gy": lax.rem(me_y + i, ngy)}, device_id_type=MESH)
        return 0

    lax.fori_loop(1, ngx, greet_x, 0)
    lax.fori_loop(1, ngy, greet_y, 0)

    eye = jnp.where(
        lax.broadcasted_iota(jnp.int32, (rank, rank), 0) == lax.broadcasted_iota(jnp.int32, (rank, rank), 1), 1.0, 0.0
    )
    lane = lax.broadcasted_iota(jnp.int32, (rank, 128), 1)
    zpos = lax.rem(lane, zlen)
    group = lane // zlen

    def at(q):
        return slice(slab * q, slab * q + slab)

    def block(i):
        return slice(rank * i, rank * i + rank)

    def cut(a):
        return [a[:, 128 * i : 128 * i + 128] for i in range(a.shape[1] // 128)]

    def roll(a, s):
        s = s % 128
        return a if s == 0 else pltpu.roll(a, s, 1)

    def from_y_before(a, halo, q):
        last = roll(halo, zlen * (-q))
        out = []
        for piece in [roll(piece, zlen) for piece in cut(a)]:
            out.append(jnp.where(lane < zlen, last, piece))
            last = piece
        return jnp.concatenate(out, axis=1)

    def from_y_after(a, halo, q):
        rolled = [roll(piece, -zlen) for piece in cut(a)] + [roll(halo, 128 - zlen - zlen * q)]
        return jnp.concatenate(
            [jnp.where(lane < 128 - zlen, rolled[i], rolled[i + 1]) for i in range(len(rolled) - 1)], axis=1
        )

    def from_z_before(a):
        return jnp.concatenate([jnp.where(zpos == 0, roll(p, 1 - zlen), roll(p, 1)) for p in cut(a)], axis=1)

    def from_z_after(a):
        return jnp.concatenate([jnp.where(zpos == zlen - 1, roll(p, zlen - 1), roll(p, -1)) for p in cut(a)], axis=1)

    def faces(ref, e):
        first, last = jnp.zeros((rank, 128), F32), jnp.zeros((rank, 128), F32)
        for q in range(slabs):
            low = ref[:, slab * q : slab * q + 128]
            high = ref[:, slab * q + slab - 128 : slab * q + slab]
            first = jnp.where(group == q, roll(low, zlen * q), first)
            last = jnp.where(group == q, roll(high, zlen * q - (128 - zlen)), last)
        yface_s[e, 0] = first
        yface_s[e, 1] = last

    def halo_copies(ref, e):
        left = {"gx": lax.rem(me_x + ngx - 1, ngx), "gy": me_y}
        right = {"gx": lax.rem(me_x + 1, ngx), "gy": me_y}
        under = {"gx": me_x, "gy": lax.rem(me_y + ngy - 1, ngy)}
        over = {"gx": me_x, "gy": lax.rem(me_y + 1, ngy)}
        plan = [
            (ref.at[:, pl.ds(0, slab)], xhalo_s.at[e, 1], left),
            (ref.at[:, pl.ds(nloc - slab, slab)], xhalo_s.at[e, 0], right),
            (yface_s.at[e, 1], yhalo_s.at[e, 0], over),
            (yface_s.at[e, 0], yhalo_s.at[e, 1], under),
        ]
        return [
            pltpu.make_async_remote_copy(
                src_ref=src, dst_ref=dst, send_sem=hsend.at[e, i], recv_sem=hrecv.at[e, i], device_id=to, device_id_type=MESH
            )
            for i, (src, dst, to) in enumerate(plan)
        ]

    def phase_copy(a, phase, i, arriving):
        mine, n = (me_x, ngx) if phase == 1 else (me_y, ngy)
        other = lax.rem(mine + i, n)
        ids = {"gx": other, "gy": me_y} if phase == 1 else {"gx": me_x, "gy": other}
        src = pay_s.at[a, other] if phase == 0 else (c_s if phase == 1 else f_s).at[a]
        slot = other if arriving else mine
        return pltpu.make_async_remote_copy(
            src_ref=src, dst_ref=(r1_s, r2_s, r3_s)[phase].at[a, slot], send_sem=asend.at[a, phase, i],
            recv_sem=arecv.at[a, phase, slot], device_id=ids, device_id_type=MESH,
        )

    def start_phase(a, phase):
        def one(i, _):
            phase_copy(a, phase, i, False).start()
            return 0

        lax.fori_loop(1, ngx if phase == 1 else ngy, one, 0)
        if phase == 0:
            r1_s[a, me_y] = pay_s[a, me_y]
        elif phase == 1:
            r2_s[a, me_x] = c_s[a]
        else:
            r3_s[a, me_y] = f_s[a]

    def end_phase(a, phase):
        def one(i, _):
            copy = phase_copy(a, phase, i, True)
            copy.wait_recv()
            copy.wait_send()
            return 0

        lax.fori_loop(1, ngx if phase == 1 else ngy, one, 0)
        if phase == 0:
            c_s[a] = jnp.sum(r1_s[a], axis=0)
        elif phase == 1:
            f_s[a] = jnp.sum(r2_s[a], axis=0)

    def pack(a, raw):
        pay_s[a] = jnp.concatenate([raw[: 2 * rank], raw[2 * rank :]], axis=1).reshape(ngy, crow, 128)

    def unpack(a):
        full = r3_s[a].reshape(128, 128) * (1.0 / cells)
        return jnp.concatenate([full[:, :rank], full[:, rank:]], axis=0)

    def tables_of(ref):
        total = jnp.zeros((6 * rank + 16, rank), F32)
        for i in range(no // 512):
            v = ref[:, 512 * i : 512 * i + 512]
            v_hi, v_lo = split(v)
            d = d_ref[:, 512 * i : 512 * i + 512]
            parts = [v * jnp.maximum(sign * d[dim : dim + 1], 0.0) for dim, sign in signs]
            l_hi, l_lo = split(jnp.concatenate(parts + [jnp.ones((16, 512), F32)], axis=0))
            total = total + gram3(l_hi, l_lo, v_hi, v_lo)
        total = total * (1.0 / no)
        return total[: 6 * rank], total[6 * rank : 6 * rank + 1]

    def column(row):
        return jnp.sum(eye * row, axis=1, keepdims=True)

    def flux(k, u_col):
        density = jnp.sum(k * u_col, axis=0, keepdims=True)
        return density, speed_of(density) * k

    def prepare(u_col):
        for q in range(slabs):
            density, g = flux(k_s[:, at(q)], u_col)
            den_s[:, at(q)] = density
            g3_s[:, at(q)] = right3(g)

    def prepare_halo(u_col):
        for i in range(2):
            g3_s[:, nloc + slab * i : nloc + slab * (i + 1)] = right3(flux(khx_s[i], u_col)[1])
            at_y = nloc + 2 * slab + 128 * i
            g3_s[:, at_y : at_y + 128] = right3(flux(khy_s[i], u_col)[1])

    st = left3(mm(eye, s_ref[...], NT))
    first_halo = halo_copies(k_s, 0)
    for q in (0, slabs - 1) + tuple(range(1, slabs - 1)):
        x_hi, x_lo = split(x_ref[at(q), :])
        k_s[:, at(q)] = bdot(st[:, :rank], x_hi, NT) + bdot(st[:, rank : 2 * rank], x_lo, NT) + bdot(st[:, 2 * rank :], x_hi, NT)
    faces(k_s, 0)
    pl.semaphore_wait(barrier, ngx + ngy - 2)
    for copy in first_halo:
        copy.start()
    tables, u_row = tables_of(v_ref)
    u_col = column(u_row)
    weights = tables
    prepare(u_col)
    for copy in first_halo:
        copy.wait()
    for i in range(2):
        khx_s[i] = xhalo_s[0, i]
        khy_s[i] = yhalo_s[0, i]
    prepare_halo(u_col)
    k_left = None
    v_now = v_ref

    for step in range(STEPS):
        last_step = step == STEPS - 1
        center = weights[block(0)] + weights[block(1)] + weights[block(2)]
        center = center + weights[block(3)] + weights[block(4)] + weights[block(5)]
        stencil = left3(c * jnp.concatenate([center, weights], axis=0))
        bx = nloc
        by = nloc + 2 * slab
        tpx_s[:, :slab] = bdot(stencil[block(1)], g3_s[:, bx : bx + slab])
        tmx_s[:, slab * slabs :] = bdot(stencil[block(3)], g3_s[:, bx + slab : bx + 2 * slab])
        tpy = bdot(stencil[block(2)], g3_s[:, by : by + 128])
        tmy = bdot(stencil[block(4)], g3_s[:, by + 128 : by + 256])
        for q in range(slabs):
            k = k_s[:, at(q)]
            if k_left is not None:
                k = bdot(k_left, right3(k))
            out = bdot(stencil, g3_s[:, at(q)])
            base_s[:, at(q)] = (1.0 - t) * k + t * u_col * den_s[:, at(q)] - out[:rank]
            tpx_s[:, at(q + 1)] = out[block(1)]
            t_s[0, :, at(q)] = out[block(2)]
            tmx_s[:, at(q)] = out[block(3)]
            t_s[1, :, at(q)] = out[block(4)]
            t_s[2, :, at(q)] = out[block(5)]
            t_s[3, :, at(q)] = out[block(6)]
        halo = halo_copies(k1_s, step + 1)
        for q in (0, slabs - 1) + tuple(range(1, slabs - 1)):
            k1_s[:, at(q)] = (
                base_s[:, at(q)]
                + tpx_s[:, at(q)]
                + tmx_s[:, at(q + 1)]
                + from_y_before(t_s[0, :, at(q)], tpy, q)
                + from_y_after(t_s[1, :, at(q)], tmy, q)
                + from_z_before(t_s[2, :, at(q)])
                + from_z_after(t_s[3, :, at(q)])
            )
            if q == 0:
                halo[0].start()
            elif q == slabs - 1:
                halo[1].start()
        faces(k1_s, step + 1)
        halo[2].start()
        halo[3].start()

        first, second = 2 * step, 2 * step + 1
        raw = jnp.zeros((3 * rank, rank), F32)
        for q in range(slabs):
            k1 = k1_s[:, at(q)]
            h = flux(k1, u_col)[1]
            h_s[:, at(q + 1)] = h
            l_hi, l_lo = split(jnp.concatenate([k1, h - from_z_before(h), from_z_after(h) - h], axis=0))
            kk_s[:rank, at(q)] = l_hi[:rank]
            kk_s[rank:, at(q)] = l_lo[:rank]
            raw = raw + gram3(l_hi, l_lo, l_hi[:rank], l_lo[:rank])
        pack(first, jnp.concatenate([raw, jnp.zeros((rank, rank), F32)], axis=0))
        start_phase(first, 0)
        for copy in halo:
            copy.wait()
        h_s[:, :slab] = flux(xhalo_s[step + 1, 0], u_col)[1]
        h_s[:, slab * (slabs + 1) :] = flux(xhalo_s[step + 1, 1], u_col)[1]
        hy = [flux(yhalo_s[step + 1, i], u_col)[1] for i in range(2)]
        raw = jnp.zeros((4 * rank, rank), F32)
        for q in range(slabs):
            h = h_s[:, at(q + 1)]
            l_hi, l_lo = split(
                jnp.concatenate(
                    [
                        h - h_s[:, at(q)],
                        h - from_y_before(h, hy[0], q),
                        h_s[:, at(q + 2)] - h,
                        from_y_after(h, hy[1], q) - h,
                    ],
                    axis=0,
                )
            )
            raw = raw + gram3(l_hi, l_lo, kk_s[:rank, at(q)], kk_s[rank:, at(q)])
        pack(second, raw)
        start_phase(second, 0)
        for phase in range(2):
            for a in (first, second):
                end_phase(a, phase)
                start_phase(a, phase + 1)
        end_phase(first, 2)
        total = unpack(first)
        upper, inverse = finish(advance(begin(total[:rank]), 0, rank // 8))
        inverse_t = mm(eye, inverse, NT)
        q_z = mm(inverse, total[rank : 3 * rank], NT)
        signed = jnp.concatenate([tables[: 2 * rank], -tables[2 * rank : 4 * rank], tables[block(4)], -tables[block(5)]], axis=0)
        s_start = (1.0 + t) * upper - t * (jnp.sum(upper * u_row, axis=1, keepdims=True) * u_row)
        s_start = s_start + c * mm(q_z, signed[4 * rank :])
        left = left3(inverse)
        for q in range(slabs):
            x1 = bdot(left, right3(k1_s[:, at(q)]))
            if last_step:
                x_out[at(q), :] = jnp.concatenate([x1, x1], axis=0).T[:, :rank]
            else:
                k_s[:, at(q)] = x1
        if not last_step:
            for i in range(2):
                khx_s[i] = bdot(left, right3(xhalo_s[step + 1, i]))
                khy_s[i] = bdot(left, right3(yhalo_s[step + 1, i]))
        end_phase(second, 2)
        q_xy = mm(inverse, unpack(second), NT)
        s2 = s_start + c * mm(q_xy, signed[: 4 * rank])
        wide = jnp.concatenate([q_xy, q_z], axis=1)
        q_stack = jnp.concatenate([wide[:, block(i)] for i in range(6)], axis=0)
        ms2 = mm(q_stack, mm(inverse_t, s2))
        mean = jnp.sum(s2 * u_row, axis=1, keepdims=True)
        left = left3(jnp.concatenate([(1.0 - t) * s2, c * ms2], axis=0))
        gram = jnp.zeros((rank, rank), F32)
        for i in range(no // 512):
            here = slice(512 * i, 512 * i + 512)
            out = bdot(left, right3(v_now[:, here]))
            d = d_ref[:, here]
            l1 = out[:rank] + t * mean
            for j, (dim, sign) in enumerate(signs):
                l1 = l1 - (sign * jnp.maximum(sign * d[dim : dim + 1], 0.0)) * out[block(j + 1)]
            v_s[:, here] = l1
            hi, lo = split(l1)
            gram = gram + gram3(hi, lo, hi, lo)
        v_now = v_s
        v_upper, v_inverse = finish(advance(begin(gram * (1.0 / no)), 0, rank // 8))
        if last_step:
            left = left3(v_inverse)
            for i in range(no // 512):
                here = slice(512 * i, 512 * i + 512)
                v_out[:, here] = bdot(left, right3(v_s[:, here]))
            s_out[...] = mm(eye, v_upper, NT)
        else:
            raw_tables, raw_row = tables_of(v_s)
            raw_col = column(raw_row)
            prepare(raw_col)
            prepare_halo(raw_col)
            left = left3(v_inverse)
            wide = mm(v_inverse, raw_tables, NT)
            weights = jnp.concatenate([wide[:, block(i)] for i in range(6)], axis=0)
            tables = mm(weights, v_inverse, NT)
            u_col = jnp.sum(v_inverse * raw_row, axis=1, keepdims=True)
            u_row = jnp.sum(eye * u_col, axis=0, keepdims=True)
            k_left = left3(v_upper)
            for i in range(no // 512):
                here = slice(512 * i, 512 * i + 512)
                v_s[:, here] = bdot(left, right3(v_s[:, here]))


def solution(mesh):
    ngx, ngy = mesh.shape["gx"], mesh.shape["gy"]

    def shards(spatial, coupling, orient, directions):
        slabs, ylen, zlen, rank = spatial.shape
        slab = ylen * zlen
        nloc = slabs * slab
        no = orient.shape[0]
        crow = 128 // ngy
        vmem = pl.BlockSpec(memory_space=pltpu.VMEM)
        sums = 2 * STEPS
        scratch = [
            (rank, nloc), (rank, nloc), (rank, nloc + slab), (rank, nloc + slab), (4, rank, nloc), (rank, nloc),
            (rank, nloc + 2 * slab), (2, rank, slab), (2, rank, 128), (rank, no),
            (STEPS + 1, 2, rank, 128), (STEPS + 1, 2, rank, slab), (STEPS + 1, 2, rank, 128),
            (sums, ngy, crow, 128), (sums, ngy, crow, 128), (sums, crow, 128), (sums, ngx, crow, 128),
            (sums, crow, 128), (sums, ngy, crow, 128), (1, nloc),
        ]
        n = max(ngx, ngy)
        x, s, v = pl.pallas_call(
            functools.partial(kernel, (ngx, ngy, slabs, ylen, zlen)),
            out_shape=(
                jax.ShapeDtypeStruct((nloc, rank), F32),
                jax.ShapeDtypeStruct((rank, rank), F32),
                jax.ShapeDtypeStruct((rank, no), F32),
            ),
            in_specs=[vmem] * 4,
            out_specs=(vmem, vmem, vmem),
            scratch_shapes=[pltpu.VMEM(shape, F32) for shape in scratch]
            + [
                pltpu.VMEM((3 * rank, nloc + 2 * slab + 256), BF16),
                pltpu.VMEM((2 * rank, nloc), BF16),
                pltpu.SemaphoreType.DMA((STEPS + 1, 4)),
                pltpu.SemaphoreType.DMA((STEPS + 1, 4)),
                pltpu.SemaphoreType.DMA((sums, 3, n)),
                pltpu.SemaphoreType.DMA((sums, 3, n)),
            ],
            compiler_params=pltpu.CompilerParams(
                collective_id=0, has_side_effects=True, vmem_limit_bytes=40 * 1024 * 1024
            ),
        )(spatial.reshape(nloc, rank), coupling, orient.T, directions)
        return x.reshape(spatial.shape), s, v.T

    return jax.shard_map(
        shards,
        mesh=mesh,
        in_specs=(P("gx", "gy", None, None), P(), P(), P()),
        out_specs=(P("gx", "gy", None, None), P(), P()),
        check_vma=False,
    )
```

time: 111 us -> 84.2 us (0.76)
  Pallas kernels: 104 us -> 77.1 us
    pallas_call x1, Pallas kernels: 104 us -> 77.1 us  [shards(): pl.pallas_call(functools.partial(kernel, (ngx, ngy, slabs, ylen, zlen)),...]
    unnamed x8 -> x11, local copies, waits for them, and re-layouts: 6.37 us -> 6.15 us
where the time goes in v1:
time: 84.2 us; the launch traced here: 83.9 us
  Pallas kernels  77.1 us (92%)
  local copies, waits for them, and re-layouts  6.15 us (7%)
    pallas_call x1, Pallas kernels, shards(): pl.pallas_call(functools.partial(kernel, (ngx, ngy, slabs, ylen, zlen)),...  77.1 us
    unnamed x11, local copies, waits for them, and re-layouts  6.15 us

profile of v1, /device:TPU:1, one launch (start us, length us, event | category | flops | bytes accessed | tf_op | source)
XLA Modules:
  0.0 83.9 jit_solution(14673797467133289810)
XLA Ops:
  0.6 0.0 copy-start
  0.6 1.2 %copy-done = f32[4,16,32,64]{3,2,1,0:T(8,128)S(1)} copy-done((f32[4,16,32,64]{3,2,1,0:T(8,128)S(1)}, f32[4,16,32,64]{3,2,1,0:T(8,128)}, u32[]{:S(2)}) %copy-start) | copy-done | bytes 524312
  1.9 0.0 copy-start.1
  1.9 1.0 %copy-done.1 = f32[2048,64]{0,1:T(8,128)S(1)} copy-done((f32[2048,64]{0,1:T(8,128)S(1)}, f32[2048,64]{0,1:T(8,128)}, u32[]{:S(2)}) %copy-start.1) | copy-done | bytes 524312
  2.9 0.0 copy-start.2
  2.9 0.8 copy-done.2
  3.7 0.0 copy-start.3
  3.7 0.8 copy-done.3
  4.4 77.1 %shard_map.67 = (f32[2048,64]{1,0:T(8,128)S(1)}, f32[64,64]{1,0:T(8,128)S(1)}, f32[64,2048]{1,0:T(8,128)S(1)}) custom-call(f32[2048,64]{1,0:T(8,128)S(1)} %bitcast.4, f32[64,64]{1,0:T(8,128)S(1)} %copy-done.2, f32[64,2048]{1,0:T(8,128)S(1)} %bitcast.6, f32[3,2048]{1,0:T(4,128)S(1)} %copy-done.3), custom_call_target="tpu_custom_call" | custom-call | tf_op jit(solution)/shard_map/pallas_call | solution.py:463
  81.6 1.0 %copy.10 = f32[4,16,32,64]{3,2,1,0:T(8,128)} copy(f32[4,16,32,64]{3,2,1,0:T(8,128)S(1)} %bitcast.5) | data formatting | bytes 1048576
  82.5 0.6 copy.11
  83.1 0.8 copy.12
Async XLA Ops:
  0.6 1.2 %copy-start = (f32[4,16,32,64]{3,2,1,0:T(8,128)S(1)}, f32[4,16,32,64]{3,2,1,0:T(8,128)}, u32[]{:S(2)}) copy-start(f32[4,16,32,64]{3,2,1,0:T(8,128)} %param.4) | copy-start | bytes 1572868
  1.9 1.0 %copy-start.1 = (f32[2048,64]{0,1:T(8,128)S(1)}, f32[2048,64]{0,1:T(8,128)}, u32[]{:S(2)}) copy-start(f32[2048,64]{0,1:T(8,128)} %param.6) | copy-start | bytes 1572868
  2.9 0.8 copy-start.2
  3.7 0.8 copy-start.3

commit v2 on v1

--- a/solution.py
+++ b/solution.py
@@ -104,16 +104,16 @@
 
 
 def kernel(
-    sizes, x_ref, s_ref, v_ref, d_ref, x_out, s_out, v_out,
+    sizes, x_hbm, s_hbm, v_hbm, d_hbm, x_out, s_out, v_out, x_ref, s_ref, v_ref, d_ref,
     k_s, base_s, tpx_s, tmx_s, t_s, k1_s, h_s, khx_s, khy_s, v_s, yface_s,
-    xhalo_s, yhalo_s, pay_s, r1_s, c_s, r2_s, f_s, r3_s, den_s, g3_s, kk_s,
-    hsend, hrecv, asend, arecv,
+    xhalo_s, yhalo_s, pay_s, r1_s, c_s, r2_s, f_s, r3_s, den_s, g3_s, kk_s, hh_s,
+    isem, hsend, hrecv, asend, arecv,
 ):
     ngx, ngy, slabs, ylen, zlen = sizes
     slab = ylen * zlen
     nloc = slabs * slab
     cells = float(nloc * ngx * ngy)
-    no = v_ref.shape[1]
+    no = v_hbm.shape[1]
     rank = 64
     c, t = courant, tumble
     me_x, me_y = lax.axis_index("gx"), lax.axis_index("gy")
@@ -132,6 +132,16 @@
 
     lax.fori_loop(1, ngx, greet_x, 0)
     lax.fori_loop(1, ngy, greet_y, 0)
+
+    order = (0, slabs - 1) + tuple(range(1, slabs - 1))
+    inputs = [pltpu.make_async_copy(s_hbm, s_ref, isem.at[0])]
+    for q in order:
+        rows = pl.ds(slab * q, slab)
+        inputs.append(pltpu.make_async_copy(x_hbm.at[rows], x_ref.at[rows], isem.at[1 + q]))
+    inputs.append(pltpu.make_async_copy(v_hbm, v_ref, isem.at[slabs + 1]))
+    inputs.append(pltpu.make_async_copy(d_hbm, d_ref, isem.at[slabs + 2]))
+    for copy in inputs:
+        copy.start()
 
     eye = jnp.where(
         lax.broadcasted_iota(jnp.int32, (rank, rank), 0) == lax.broadcasted_iota(jnp.int32, (rank, rank), 1), 1.0, 0.0
@@ -153,16 +163,17 @@
         s = s % 128
         return a if s == 0 else pltpu.roll(a, s, 1)
 
-    def from_y_before(a, halo, q):
-        last = roll(halo, zlen * (-q))
+    def from_y_before(a, halo=None, q=0):
+        last = 0.0 if halo is None else roll(halo, zlen * (-q))
         out = []
         for piece in [roll(piece, zlen) for piece in cut(a)]:
             out.append(jnp.where(lane < zlen, last, piece))
             last = piece
         return jnp.concatenate(out, axis=1)
 
-    def from_y_after(a, halo, q):
-        rolled = [roll(piece, -zlen) for piece in cut(a)] + [roll(halo, 128 - zlen - zlen * q)]
+    def from_y_after(a, halo=None, q=0):
+        rolled = [roll(piece, -zlen) for piece in cut(a)]
+        rolled.append(0.0 if halo is None else roll(halo, 128 - zlen - zlen * q))
         return jnp.concatenate(
             [jnp.where(lane < 128 - zlen, rolled[i], rolled[i + 1]) for i in range(len(rolled) - 1)], axis=1
         )
@@ -201,23 +212,20 @@
             for i, (src, dst, to) in enumerate(plan)
         ]
 
-    def phase_copy(a, phase, i, arriving):
+    landing = (r1_s, r2_s, r3_s)
+
+    def start_phase(a, phase):
         mine, n = (me_x, ngx) if phase == 1 else (me_y, ngy)
-        other = lax.rem(mine + i, n)
-        ids = {"gx": other, "gy": me_y} if phase == 1 else {"gx": me_x, "gy": other}
-        src = pay_s.at[a, other] if phase == 0 else (c_s if phase == 1 else f_s).at[a]
-        slot = other if arriving else mine
-        return pltpu.make_async_remote_copy(
-            src_ref=src, dst_ref=(r1_s, r2_s, r3_s)[phase].at[a, slot], send_sem=asend.at[a, phase, i],
-            recv_sem=arecv.at[a, phase, slot], device_id=ids, device_id_type=MESH,
-        )
-
-    def start_phase(a, phase):
-        def one(i, _):
-            phase_copy(a, phase, i, False).start()
-            return 0
-
-        lax.fori_loop(1, ngx if phase == 1 else ngy, one, 0)
+        for i in sorted(range(1, n), key=lambda i: -min(i, n - i)):
+            other = lax.rem(mine + i, n)
+            pltpu.make_async_remote_copy(
+                src_ref=pay_s.at[a, other] if phase == 0 else (c_s if phase == 1 else f_s).at[a],
+                dst_ref=landing[phase].at[a, mine],
+                send_sem=asend.at[a, phase],
+                recv_sem=arecv.at[a, phase],
+                device_id={"gx": other, "gy": me_y} if phase == 1 else {"gx": me_x, "gy": other},
+                device_id_type=MESH,
+            ).start()
         if phase == 0:
             r1_s[a, me_y] = pay_s[a, me_y]
         elif phase == 1:
@@ -225,14 +233,12 @@
         else:
             r3_s[a, me_y] = f_s[a]
 
+    def all_of(a, phase, sem):
+        part = landing[phase].at[a, pl.ds(0, (ngx if phase == 1 else ngy) - 1)]
+        return pltpu.make_async_copy(part, part, sem.at[a, phase])
+
     def end_phase(a, phase):
-        def one(i, _):
-            copy = phase_copy(a, phase, i, True)
-            copy.wait_recv()
-            copy.wait_send()
-            return 0
-
-        lax.fori_loop(1, ngx if phase == 1 else ngy, one, 0)
+        all_of(a, phase, arecv).wait()
         if phase == 0:
             c_s[a] = jnp.sum(r1_s[a], axis=0)
         elif phase == 1:
@@ -276,15 +282,19 @@
             at_y = nloc + 2 * slab + 128 * i
             g3_s[:, at_y : at_y + 128] = right3(flux(khy_s[i], u_col)[1])
 
+    inputs[0].wait()
     st = left3(mm(eye, s_ref[...], NT))
     first_halo = halo_copies(k_s, 0)
-    for q in (0, slabs - 1) + tuple(range(1, slabs - 1)):
+    for i, q in enumerate(order):
+        inputs[1 + i].wait()
         x_hi, x_lo = split(x_ref[at(q), :])
         k_s[:, at(q)] = bdot(st[:, :rank], x_hi, NT) + bdot(st[:, rank : 2 * rank], x_lo, NT) + bdot(st[:, 2 * rank :], x_hi, NT)
     faces(k_s, 0)
     pl.semaphore_wait(barrier, ngx + ngy - 2)
     for copy in first_halo:
         copy.start()
+    inputs[slabs + 1].wait()
+    inputs[slabs + 2].wait()
     tables, u_row = tables_of(v_ref)
     u_col = column(u_row)
     weights = tables
@@ -297,6 +307,7 @@
     prepare_halo(u_col)
     k_left = None
     v_now = v_ref
+    later = None
 
     for step in range(STEPS):
         last_step = step == STEPS - 1
@@ -309,7 +320,9 @@
         tmx_s[:, slab * slabs :] = bdot(stencil[block(3)], g3_s[:, bx + slab : bx + 2 * slab])
         tpy = bdot(stencil[block(2)], g3_s[:, by : by + 128])
         tmy = bdot(stencil[block(4)], g3_s[:, by + 128 : by + 256])
-        for q in range(slabs):
+        halo = halo_copies(k1_s, step + 1)
+
+        def spread(q):
             k = k_s[:, at(q)]
             if k_left is not None:
                 k = bdot(k_left, right3(k))
@@ -321,8 +334,8 @@
             t_s[1, :, at(q)] = out[block(4)]
             t_s[2, :, at(q)] = out[block(5)]
             t_s[3, :, at(q)] = out[block(6)]
-        halo = halo_copies(k1_s, step + 1)
-        for q in (0, slabs - 1) + tuple(range(1, slabs - 1)):
+
+        def combine(q):
             k1_s[:, at(q)] = (
                 base_s[:, at(q)]
                 + tpx_s[:, at(q)]
@@ -332,47 +345,63 @@
                 + from_z_before(t_s[2, :, at(q)])
                 + from_z_after(t_s[3, :, at(q)])
             )
-            if q == 0:
-                halo[0].start()
-            elif q == slabs - 1:
-                halo[1].start()
+
+        spread(0)
+        spread(1)
+        combine(0)
+        halo[0].start()
+        for q in range(slabs - 1, 1, -1):
+            spread(q)
+        combine(slabs - 1)
+        halo[1].start()
+        for q in range(1, slabs - 1):
+            combine(q)
         faces(k1_s, step + 1)
         halo[2].start()
         halo[3].start()
 
         first, second = 2 * step, 2 * step + 1
-        raw = jnp.zeros((3 * rank, rank), F32)
+        raw = jnp.zeros((4 * rank, rank), F32)
         for q in range(slabs):
             k1 = k1_s[:, at(q)]
             h = flux(k1, u_col)[1]
-            h_s[:, at(q + 1)] = h
-            l_hi, l_lo = split(jnp.concatenate([k1, h - from_z_before(h), from_z_after(h) - h], axis=0))
-            kk_s[:rank, at(q)] = l_hi[:rank]
-            kk_s[rank:, at(q)] = l_lo[:rank]
+            h_s[:, at(q)] = h
+            l_hi, l_lo = split(jnp.concatenate([k1, h - from_z_before(h), from_z_after(h) - h, h], axis=0))
+            kk_s[0, :, at(q)], kk_s[1, :, at(q)] = l_hi[:rank], l_lo[:rank]
+            hh_s[0, :, at(q)], hh_s[1, :, at(q)] = l_hi[3 * rank :], l_lo[3 * rank :]
             raw = raw + gram3(l_hi, l_lo, l_hi[:rank], l_lo[:rank])
-        pack(first, jnp.concatenate([raw, jnp.zeros((rank, rank), F32)], axis=0))
+        pack(first, raw)
         start_phase(first, 0)
+        h_k1 = raw[3 * rank :]
+        if later is not None:
+            tables = later()
+
+        sums = {name: jnp.zeros((rank, rank), F32) for name in ("x-", "y-", "x+", "y+")}
+        for q in range(slabs):
+            h = h_s[:, at(q)]
+            y_hi, y_lo = split(jnp.concatenate([from_y_before(h), from_y_after(h)], axis=0))
+            names, his, los = ["y-", "y+"], [y_hi], [y_lo]
+            for name, other in (("x-", q - 1), ("x+", q + 1)):
+                if 0 <= other < slabs:
+                    names.append(name)
+                    his.append(hh_s[0, :, at(other)])
+                    los.append(hh_s[1, :, at(other)])
+            out = gram3(jnp.concatenate(his, axis=0), jnp.concatenate(los, axis=0), kk_s[0, :, at(q)], kk_s[1, :, at(q)])
+            for i, name in enumerate(names):
+                sums[name] = sums[name] + out[block(i)]
+        y_first, y_last = split(yface_s[step + 1, 0]), split(yface_s[step + 1, 1])
         for copy in halo:
             copy.wait()
-        h_s[:, :slab] = flux(xhalo_s[step + 1, 0], u_col)[1]
-        h_s[:, slab * (slabs + 1) :] = flux(xhalo_s[step + 1, 1], u_col)[1]
-        hy = [flux(yhalo_s[step + 1, i], u_col)[1] for i in range(2)]
-        raw = jnp.zeros((4 * rank, rank), F32)
-        for q in range(slabs):
-            h = h_s[:, at(q + 1)]
-            l_hi, l_lo = split(
-                jnp.concatenate(
-                    [
-                        h - h_s[:, at(q)],
-                        h - from_y_before(h, hy[0], q),
-                        h_s[:, at(q + 2)] - h,
-                        from_y_after(h, hy[1], q) - h,
-                    ],
-                    axis=0,
-                )
-            )
-            raw = raw + gram3(l_hi, l_lo, kk_s[:rank, at(q)], kk_s[rank:, at(q)])
-        pack(second, raw)
+        for i, (name, edge) in enumerate((("x-", 0), ("x+", slabs - 1))):
+            hi, lo = split(flux(xhalo_s[step + 1, i], u_col)[1])
+            sums[name] = sums[name] + gram3(hi, lo, kk_s[0, :, at(edge)], kk_s[1, :, at(edge)])
+        for i, (name, edge) in enumerate((("y-", y_first), ("y+", y_last))):
+            hi, lo = split(flux(yhalo_s[step + 1, i], u_col)[1])
+            sums[name] = sums[name] + gram3(hi, lo, *edge)
+        pack(
+            second,
+            jnp.concatenate([h_k1 - sums["x-"], h_k1 - sums["y-"], sums["x+"] - h_k1, sums["y+"] - h_k1], axis=0),
+        )
         start_phase(second, 0)
         for phase in range(2):
             for a in (first, second):
@@ -432,13 +461,33 @@
             left = left3(v_inverse)
             wide = mm(v_inverse, raw_tables, NT)
             weights = jnp.concatenate([wide[:, block(i)] for i in range(6)], axis=0)
-            tables = mm(weights, v_inverse, NT)
             u_col = jnp.sum(v_inverse * raw_row, axis=1, keepdims=True)
             u_row = jnp.sum(eye * u_col, axis=0, keepdims=True)
             k_left = left3(v_upper)
-            for i in range(no // 512):
-                here = slice(512 * i, 512 * i + 512)
-                v_s[:, here] = bdot(left, right3(v_s[:, here]))
+
+            def later(left=left, weights=weights, v_inverse=v_inverse):
+                for i in range(no // 512):
+                    here = slice(512 * i, 512 * i + 512)
+                    v_s[:, here] = bdot(left, right3(v_s[:, here]))
+                return mm(weights, v_inverse, NT)
+
+    def drain(a, _):
+        for phase in range(3):
+            all_of(a, phase, asend).wait()
+        return 0
+
+    lax.fori_loop(0, 2 * STEPS, drain, 0)
+
+
+def store(x_ref, s_ref, v_ref, x_out, s_out, v_out, sems):
+    copies = [
+        pltpu.make_async_copy(src, dst, sems.at[i])
+        for i, (src, dst) in enumerate(((x_ref, x_out), (v_ref, v_out), (s_ref, s_out)))
+    ]
+    for copy in copies:
+        copy.start()
+    for copy in copies:
+        copy.wait()
 
 
 def solution(mesh):
@@ -450,38 +499,49 @@
         nloc = slabs * slab
         no = orient.shape[0]
         crow = 128 // ngy
-        vmem = pl.BlockSpec(memory_space=pltpu.VMEM)
+        vmem, hbm = pl.BlockSpec(memory_space=pltpu.VMEM), pl.BlockSpec(memory_space=pltpu.HBM)
         sums = 2 * STEPS
         scratch = [
+            (nloc, rank), (rank, rank), (rank, no), (3, no),
             (rank, nloc), (rank, nloc), (rank, nloc + slab), (rank, nloc + slab), (4, rank, nloc), (rank, nloc),
-            (rank, nloc + 2 * slab), (2, rank, slab), (2, rank, 128), (rank, no),
+            (rank, nloc), (2, rank, slab), (2, rank, 128), (rank, no),
             (STEPS + 1, 2, rank, 128), (STEPS + 1, 2, rank, slab), (STEPS + 1, 2, rank, 128),
             (sums, ngy, crow, 128), (sums, ngy, crow, 128), (sums, crow, 128), (sums, ngx, crow, 128),
             (sums, crow, 128), (sums, ngy, crow, 128), (1, nloc),
         ]
-        n = max(ngx, ngy)
-        x, s, v = pl.pallas_call(
+        outs = (
+            jax.ShapeDtypeStruct((nloc, rank), F32),
+            jax.ShapeDtypeStruct((rank, rank), F32),
+            jax.ShapeDtypeStruct((rank, no), F32),
+        )
+        results = pl.pallas_call(
             functools.partial(kernel, (ngx, ngy, slabs, ylen, zlen)),
-            out_shape=(
-                jax.ShapeDtypeStruct((nloc, rank), F32),
-                jax.ShapeDtypeStruct((rank, rank), F32),
-                jax.ShapeDtypeStruct((rank, no), F32),
-            ),
-            in_specs=[vmem] * 4,
+            out_shape=outs,
+            in_specs=[hbm] * 4,
             out_specs=(vmem, vmem, vmem),
             scratch_shapes=[pltpu.VMEM(shape, F32) for shape in scratch]
             + [
                 pltpu.VMEM((3 * rank, nloc + 2 * slab + 256), BF16),
-                pltpu.VMEM((2 * rank, nloc), BF16),
+                pltpu.VMEM((2, rank, nloc), BF16),
+                pltpu.VMEM((2, rank, nloc), BF16),
+                pltpu.SemaphoreType.DMA((slabs + 3,)),
                 pltpu.SemaphoreType.DMA((STEPS + 1, 4)),
                 pltpu.SemaphoreType.DMA((STEPS + 1, 4)),
-                pltpu.SemaphoreType.DMA((sums, 3, n)),
-                pltpu.SemaphoreType.DMA((sums, 3, n)),
+                pltpu.SemaphoreType.DMA((sums, 3)),
+                pltpu.SemaphoreType.DMA((sums, 3)),
             ],
             compiler_params=pltpu.CompilerParams(
                 collective_id=0, has_side_effects=True, vmem_limit_bytes=40 * 1024 * 1024
             ),
-        )(spatial.reshape(nloc, rank), coupling, orient.T, directions)
+        )(*[pltpu.with_memory_space_constraint(a, pltpu.HBM) for a in (spatial.reshape(nloc, rank), coupling, orient.T, directions)])
+        x, s, v = pl.pallas_call(
+            store,
+            out_shape=outs,
+            in_specs=[vmem] * 3,
+            out_specs=(hbm, hbm, hbm),
+            scratch_shapes=[pltpu.SemaphoreType.DMA((3,))],
+            compiler_params=pltpu.CompilerParams(vmem_limit_bytes=1024 * 1024),
+        )(*results)
         return x.reshape(spatial.shape), s, v.T
 
     return jax.shard_map(

time: 84.2 us -> 72.2 us (0.86)
  local copies, waits for them, and re-layouts: 6.15 us -> 0 us
  Pallas kernels: 77.1 us -> 71.3 us
    pallas_call x1, Pallas kernels: 77.1 us -> 70.1 us  [shards(): pl.pallas_call(functools.partial(kernel, (ngx, ngy, slabs, ylen, zlen)),...]
    unnamed x11 -> x0, local copies, waits for them, and re-layouts: 6.15 us -> none
    pallas_call x0 -> x1, Pallas kernels: none -> 1.17 us  [shards(): pl.pallas_call(store, out_shape=outs, in_specs=[vmem] * 3, out_specs=(hbm...]
where the time goes in v2:
time: 72.2 us; the launch traced here: 72.1 us
  Pallas kernels  71.3 us (99%)
  between operations  0.8 us (1%)
    pallas_call x1, Pallas kernels, shards(): pl.pallas_call(functools.partial(kernel, (ngx, ngy, slabs, ylen, zlen)),...  70.1 us

profile of v2, /device:TPU:1, one launch (start us, length us, event | category | flops | bytes accessed | tf_op | source)
XLA Modules:
  0.0 72.1 jit_solution(13518271015738250941)
XLA Ops:
  0.6 70.1 %shard_map.67 = (f32[2048,64]{1,0:T(8,128)S(1)}, f32[64,64]{1,0:T(8,128)S(1)}, f32[64,2048]{1,0:T(8,128)S(1)}) custom-call(f32[2048,64]{1,0:T(8,128)} %bitcast.4, f32[64,64]{1,0:T(8,128)} %s_hbm.1, f32[64,2048]{1,0:T(8,128)} %bitcast.5, f32[3,2048]{1,0:T(4,128)} %d_hbm.1), custom_call_target="tpu_custom_call" | custom-call | tf_op jit(solution)/shard_map/pallas_call | solution.py:517
  70.7 1.2 %shard_map.68 = (f32[2048,64]{1,0:T(8,128)}, f32[64,64]{1,0:T(8,128)}, f32[64,2048]{1,0:T(8,128)}) custom-call(f32[2048,64]{1,0:T(8,128)S(1)} %get-tuple-element.9.x_ref, f32[64,64]{1,0:T(8,128)S(1)} %get-tuple-element.10.s_ref, f32[64,2048]{1,0:T(8,128)S(1)} %get-tuple-element.11.v_ref), custom_call_target="tpu_custom_call" | custom-call | tf_op jit(solution)/shard_map/pallas_call | solution.py:537

commit v3 on v2

--- a/solution.py
+++ b/solution.py
@@ -41,6 +41,12 @@
     return jnp.concatenate([hi, lo, hi], axis=0)
 
 
+def mm3(a, b, dims=NN):
+    hi, lo = split(b)
+    axis = 0 if dims is NN else 1
+    return bdot(left3(a), jnp.concatenate([hi, lo, hi], axis=axis), dims)
+
+
 def gram3(left_hi, left_lo, right_hi, right_lo):
     width = right_hi.shape[0]
     first = bdot(left_hi, jnp.concatenate([right_hi, right_lo], axis=0), NT)
@@ -70,27 +76,32 @@
 
     for kb in range(start, stop):
         own = [across(blocks[kb], 8 * kb + c) for c in range(8)]
-        rows, inverses, heads = [], [], []
+        pairs = []
         current = blocks[kb]
-        for k in range(8):
-            head = {j: down(own[j], k) for j in range(k, 8)}
-            inverse = 1.0 / head[k]
-            row = down(current, k)
-            factor = jnp.where(below > k, own[k] * inverse, 0.0)
-            for j in range(k + 1, 8):
-                own[j] = own[j] - factor * head[j]
-            current = current - factor * row
-            rows.append(row)
-            inverses.append(inverse)
-            heads.append(head)
+        for k in range(0, 8, 2):
+            first = {j: down(own[j], k) for j in range(k, 8)}
+            second = {j: down(own[j], k + 1) for j in range(k + 1, 8)}
+            a, b, d = first[k], first[k + 1], second[k + 1]
+            inverse = 1.0 / (a * d - b * b)
+            p, q, r = d * inverse, b * inverse, a * inverse
+            rows = down(current, k), down(current, k + 1)
+            f1 = jnp.where(below > k + 1, own[k] * p - own[k + 1] * q, 0.0)
+            f2 = jnp.where(below > k + 1, own[k + 1] * r - own[k] * q, 0.0)
+            for j in range(k + 2, 8):
+                own[j] = own[j] - f1 * first[j] - f2 * second[j]
+            f1 = jnp.where(below == k + 1, b / a, f1)
+            current = current - f1 * rows[0] - f2 * rows[1]
+            pairs.append((p, q, r, rows, first, second))
         blocks[kb] = current
         for b in range(kb + 1, len(blocks)):
             columns = [across(blocks[b], 8 * kb + c) for c in range(8)]
-            for k in range(8):
-                factor = columns[k] * inverses[k]
-                for j in range(k + 1, 8):
-                    columns[j] = columns[j] - factor * heads[k][j]
-                blocks[b] = blocks[b] - factor * rows[k]
+            for i, (p, q, r, rows, first, second) in enumerate(pairs):
+                k = 2 * i
+                f1 = columns[k] * p - columns[k + 1] * q
+                f2 = columns[k + 1] * r - columns[k] * q
+                for j in range(k + 2, 8):
+                    columns[j] = columns[j] - f1 * first[j] - f2 * second[j]
+                blocks[b] = blocks[b] - f1 * rows[0] - f2 * rows[1]
     return blocks
 
 
@@ -120,19 +131,6 @@
     crow = 128 // ngy
     signs = ((0, 1), (1, 1), (0, -1), (1, -1), (2, 1), (2, -1))
 
-    barrier = pltpu.get_barrier_semaphore()
-
-    def greet_x(i, _):
-        pl.semaphore_signal(barrier, inc=1, device_id={"gx": lax.rem(me_x + i, ngx), "gy": me_y}, device_id_type=MESH)
-        return 0
-
-    def greet_y(i, _):
-        pl.semaphore_signal(barrier, inc=1, device_id={"gx": me_x, "gy": lax.rem(me_y + i, ngy)}, device_id_type=MESH)
-        return 0
-
-    lax.fori_loop(1, ngx, greet_x, 0)
-    lax.fori_loop(1, ngy, greet_y, 0)
-
     order = (0, slabs - 1) + tuple(range(1, slabs - 1))
     inputs = [pltpu.make_async_copy(s_hbm, s_ref, isem.at[0])]
     for q in order:
@@ -143,6 +141,19 @@
     for copy in inputs:
         copy.start()
 
+    barrier = pltpu.get_barrier_semaphore()
+
+    def greet_x(i, _):
+        pl.semaphore_signal(barrier, inc=1, device_id={"gx": lax.rem(me_x + i, ngx), "gy": me_y}, device_id_type=MESH)
+        return 0
+
+    def greet_y(i, _):
+        pl.semaphore_signal(barrier, inc=1, device_id={"gx": me_x, "gy": lax.rem(me_y + i, ngy)}, device_id_type=MESH)
+        return 0
+
+    lax.fori_loop(1, ngx, greet_x, 0)
+    lax.fori_loop(1, ngy, greet_y, 0)
+
     eye = jnp.where(
         lax.broadcasted_iota(jnp.int32, (rank, rank), 0) == lax.broadcasted_iota(jnp.int32, (rank, rank), 1), 1.0, 0.0
     )
@@ -199,11 +210,16 @@
         right = {"gx": lax.rem(me_x + 1, ngx), "gy": me_y}
         under = {"gx": me_x, "gy": lax.rem(me_y + ngy - 1, ngy)}
         over = {"gx": me_x, "gy": lax.rem(me_y + 1, ngy)}
+        half = slab // 2
+        low, high = pl.ds(0, half), pl.ds(half, half)
+        end = nloc - slab
         plan = [
-            (ref.at[:, pl.ds(0, slab)], xhalo_s.at[e, 1], left),
-            (ref.at[:, pl.ds(nloc - slab, slab)], xhalo_s.at[e, 0], right),
+            (ref.at[:, pl.ds(half, half)], xhalo_s.at[e, 1, :, high], left),
+            (ref.at[:, pl.ds(end, half)], xhalo_s.at[e, 0, :, low], right),
             (yface_s.at[e, 1], yhalo_s.at[e, 0], over),
             (yface_s.at[e, 0], yhalo_s.at[e, 1], under),
+            (ref.at[:, pl.ds(0, half)], xhalo_s.at[e, 1, :, low], left),
+            (ref.at[:, pl.ds(end + half, half)], xhalo_s.at[e, 0, :, high], right),
         ]
         return [
             pltpu.make_async_remote_copy(
@@ -289,22 +305,19 @@
         inputs[1 + i].wait()
         x_hi, x_lo = split(x_ref[at(q), :])
         k_s[:, at(q)] = bdot(st[:, :rank], x_hi, NT) + bdot(st[:, rank : 2 * rank], x_lo, NT) + bdot(st[:, 2 * rank :], x_hi, NT)
+        if i == 1:
+            pl.semaphore_wait(barrier, ngx + ngy - 2)
+            for n in (0, 1, 4, 5):
+                first_halo[n].start()
     faces(k_s, 0)
-    pl.semaphore_wait(barrier, ngx + ngy - 2)
-    for copy in first_halo:
-        copy.start()
+    first_halo[2].start()
+    first_halo[3].start()
     inputs[slabs + 1].wait()
     inputs[slabs + 2].wait()
     tables, u_row = tables_of(v_ref)
     u_col = column(u_row)
     weights = tables
     prepare(u_col)
-    for copy in first_halo:
-        copy.wait()
-    for i in range(2):
-        khx_s[i] = xhalo_s[0, i]
-        khy_s[i] = yhalo_s[0, i]
-    prepare_halo(u_col)
     k_left = None
     v_now = v_ref
     later = None
@@ -316,10 +329,15 @@
         stencil = left3(c * jnp.concatenate([center, weights], axis=0))
         bx = nloc
         by = nloc + 2 * slab
-        tpx_s[:, :slab] = bdot(stencil[block(1)], g3_s[:, bx : bx + slab])
-        tmx_s[:, slab * slabs :] = bdot(stencil[block(3)], g3_s[:, bx + slab : bx + 2 * slab])
-        tpy = bdot(stencil[block(2)], g3_s[:, by : by + 128])
-        tmy = bdot(stencil[block(4)], g3_s[:, by + 128 : by + 256])
+
+        def halo_terms():
+            tpx_s[:, :slab] = bdot(stencil[block(1)], g3_s[:, bx : bx + slab])
+            tmx_s[:, slab * slabs :] = bdot(stencil[block(3)], g3_s[:, bx + slab : bx + 2 * slab])
+            return (
+                bdot(stencil[block(2)], g3_s[:, by : by + 128]),
+                bdot(stencil[block(4)], g3_s[:, by + 128 : by + 256]),
+            )
+
         halo = halo_copies(k1_s, step + 1)
 
         def spread(q):
@@ -346,12 +364,25 @@
                 + from_z_after(t_s[3, :, at(q)])
             )
 
-        spread(0)
-        spread(1)
+        if step == 0:
+            for q in order:
+                spread(q)
+            for copy in first_halo:
+                copy.wait()
+            for i in range(2):
+                khx_s[i] = xhalo_s[0, i]
+                khy_s[i] = yhalo_s[0, i]
+            prepare_halo(u_col)
+            tpy, tmy = halo_terms()
+        else:
+            tpy, tmy = halo_terms()
+            spread(0)
+            spread(1)
         combine(0)
         halo[0].start()
-        for q in range(slabs - 1, 1, -1):
-            spread(q)
+        if step > 0:
+            for q in range(slabs - 1, 1, -1):
+                spread(q)
         combine(slabs - 1)
         halo[1].start()
         for q in range(1, slabs - 1):
@@ -372,6 +403,9 @@
             raw = raw + gram3(l_hi, l_lo, l_hi[:rank], l_lo[:rank])
         pack(first, raw)
         start_phase(first, 0)
+        if not last_step:
+            halo[4].start()
+            halo[5].start()
         h_k1 = raw[3 * rank :]
         if later is not None:
             tables = later()
@@ -390,11 +424,28 @@
             for i, name in enumerate(names):
                 sums[name] = sums[name] + out[block(i)]
         y_first, y_last = split(yface_s[step + 1, 0]), split(yface_s[step + 1, 1])
-        for copy in halo:
+        half = slab // 2
+        low, high = slice(0, half), slice(half, slab)
+        own_low, own_high = slice(0, half), slice(nloc - half, nloc)
+        for copy in halo[:4]:
             copy.wait()
-        for i, (name, edge) in enumerate((("x-", 0), ("x+", slabs - 1))):
-            hi, lo = split(flux(xhalo_s[step + 1, i], u_col)[1])
-            sums[name] = sums[name] + gram3(hi, lo, kk_s[0, :, at(edge)], kk_s[1, :, at(edge)])
+        before, after = xhalo_s[step + 1, 0, :, low], xhalo_s[step + 1, 1, :, high]
+        b_hi, b_lo = split(before)
+        a_hi, a_lo = split(after)
+        hb_hi, hb_lo = split(flux(before, u_col)[1])
+        ha_hi, ha_lo = split(flux(after, u_col)[1])
+
+        def side(x, y):
+            return jnp.concatenate([x, y], axis=1)
+
+        sums["x-"] = sums["x-"] + gram3(
+            side(hb_hi, hh_s[0, :, own_high]), side(hb_lo, hh_s[1, :, own_high]),
+            side(kk_s[0, :, own_low], a_hi), side(kk_s[1, :, own_low], a_lo),
+        )
+        sums["x+"] = sums["x+"] + gram3(
+            side(hh_s[0, :, own_low], ha_hi), side(hh_s[1, :, own_low], ha_lo),
+            side(b_hi, kk_s[0, :, own_high]), side(b_lo, kk_s[1, :, own_high]),
+        )
         for i, (name, edge) in enumerate((("y-", y_first), ("y+", y_last))):
             hi, lo = split(flux(yhalo_s[step + 1, i], u_col)[1])
             sums[name] = sums[name] + gram3(hi, lo, *edge)
@@ -411,10 +462,10 @@
         total = unpack(first)
         upper, inverse = finish(advance(begin(total[:rank]), 0, rank // 8))
         inverse_t = mm(eye, inverse, NT)
-        q_z = mm(inverse, total[rank : 3 * rank], NT)
+        q_z = mm3(inverse, total[rank : 3 * rank], NT)
         signed = jnp.concatenate([tables[: 2 * rank], -tables[2 * rank : 4 * rank], tables[block(4)], -tables[block(5)]], axis=0)
         s_start = (1.0 + t) * upper - t * (jnp.sum(upper * u_row, axis=1, keepdims=True) * u_row)
-        s_start = s_start + c * mm(q_z, signed[4 * rank :])
+        s_start = s_start + c * mm3(q_z, signed[4 * rank :])
         left = left3(inverse)
         for q in range(slabs):
             x1 = bdot(left, right3(k1_s[:, at(q)]))
@@ -423,15 +474,17 @@
             else:
                 k_s[:, at(q)] = x1
         if not last_step:
+            halo[4].wait()
+            halo[5].wait()
             for i in range(2):
                 khx_s[i] = bdot(left, right3(xhalo_s[step + 1, i]))
                 khy_s[i] = bdot(left, right3(yhalo_s[step + 1, i]))
         end_phase(second, 2)
-        q_xy = mm(inverse, unpack(second), NT)
-        s2 = s_start + c * mm(q_xy, signed[: 4 * rank])
+        q_xy = mm3(inverse, unpack(second), NT)
+        s2 = s_start + c * mm3(q_xy, signed[: 4 * rank])
         wide = jnp.concatenate([q_xy, q_z], axis=1)
         q_stack = jnp.concatenate([wide[:, block(i)] for i in range(6)], axis=0)
-        ms2 = mm(q_stack, mm(inverse_t, s2))
+        ms2 = mm3(q_stack, mm3(inverse_t, s2))
         mean = jnp.sum(s2 * u_row, axis=1, keepdims=True)
         left = left3(jnp.concatenate([(1.0 - t) * s2, c * ms2], axis=0))
         gram = jnp.zeros((rank, rank), F32)
@@ -525,8 +578,8 @@
                 pltpu.VMEM((2, rank, nloc), BF16),
                 pltpu.VMEM((2, rank, nloc), BF16),
                 pltpu.SemaphoreType.DMA((slabs + 3,)),
-                pltpu.SemaphoreType.DMA((STEPS + 1, 4)),
-                pltpu.SemaphoreType.DMA((STEPS + 1, 4)),
+                pltpu.SemaphoreType.DMA((STEPS + 1, 6)),
+                pltpu.SemaphoreType.DMA((STEPS + 1, 6)),
                 pltpu.SemaphoreType.DMA((sums, 3)),
                 pltpu.SemaphoreType.DMA((sums, 3)),
             ],

time: 72.2 us -> 68.7 us (0.952)
  Pallas kernels: 71.3 us -> 67.8 us
    pallas_call x1, Pallas kernels: 70.1 us -> 66.7 us  [shards(): pl.pallas_call(functools.partial(kernel, (ngx, ngy, slabs, ylen, zlen)),...]
where the time goes in v3:
time: 68.7 us; the launch traced here: 68.6 us
  Pallas kernels  67.8 us (99%)
  between operations  0.8 us (1%)
    pallas_call x1, Pallas kernels, shards(): pl.pallas_call(functools.partial(kernel, (ngx, ngy, slabs, ylen, zlen)),...  66.7 us

profile of v3, /device:TPU:1, one launch (start us, length us, event | category | flops | bytes accessed | tf_op | source)
XLA Modules:
  0.0 68.6 jit_solution(7664966616822507999)
XLA Ops:
  0.6 66.7 %shard_map.67 = (f32[2048,64]{1,0:T(8,128)S(1)}, f32[64,64]{1,0:T(8,128)S(1)}, f32[64,2048]{1,0:T(8,128)S(1)}) custom-call(f32[2048,64]{1,0:T(8,128)} %bitcast.4, f32[64,64]{1,0:T(8,128)} %s_hbm.1, f32[64,2048]{1,0:T(8,128)} %bitcast.5, f32[3,2048]{1,0:T(4,128)} %d_hbm.1), custom_call_target="tpu_custom_call" | custom-call | tf_op jit(solution)/shard_map/pallas_call | solution.py:570
  67.3 1.2 %shard_map.68 = (f32[2048,64]{1,0:T(8,128)}, f32[64,64]{1,0:T(8,128)}, f32[64,2048]{1,0:T(8,128)}) custom-call(f32[2048,64]{1,0:T(8,128)S(1)} %get-tuple-element.9.x_ref, f32[64,64]{1,0:T(8,128)S(1)} %get-tuple-element.10.s_ref, f32[64,2048]{1,0:T(8,128)S(1)} %get-tuple-element.11.v_ref), custom_call_target="tpu_custom_call" | custom-call | tf_op jit(solution)/shard_map/pallas_call | solution.py:590

commit v4 on v3

--- a/solution.py
+++ b/solution.py
@@ -41,10 +41,12 @@
     return jnp.concatenate([hi, lo, hi], axis=0)
 
 
+def dot3(a, b, dims=NN):
+    return bdot(a[0], b[0], dims) + (bdot(a[0], b[1], dims) + bdot(a[1], b[0], dims))
+
+
 def mm3(a, b, dims=NN):
-    hi, lo = split(b)
-    axis = 0 if dims is NN else 1
-    return bdot(left3(a), jnp.concatenate([hi, lo, hi], axis=axis), dims)
+    return dot3(split(a), split(b), dims)
 
 
 def gram3(left_hi, left_lo, right_hi, right_lo):
@@ -74,34 +76,46 @@
     def down(a, r):
         return jnp.broadcast_to(a[r : r + 1], (8, width))
 
+    count = len(blocks)
+    own = [across(blocks[start], 8 * start + c) for c in range(8)]
     for kb in range(start, stop):
-        own = [across(blocks[kb], 8 * kb + c) for c in range(8)]
-        pairs = []
+        under = {n: [across(blocks[n], 8 * kb + c) for c in range(8)] for n in range(kb + 1, count)}
+        ahead = [across(blocks[kb + 1], 8 * kb + 8 + c) for c in range(8)] if kb + 1 < count else None
         current = blocks[kb]
+        a, b, d = down(own[0], 0), down(own[1], 0), down(own[1], 1)
         for k in range(0, 8, 2):
-            first = {j: down(own[j], k) for j in range(k, 8)}
-            second = {j: down(own[j], k + 1) for j in range(k + 1, 8)}
-            a, b, d = first[k], first[k + 1], second[k + 1]
+            first = {j: down(own[j], k) for j in range(k + 2, 8)}
+            second = {j: down(own[j], k + 1) for j in range(k + 2, 8)}
             inverse = 1.0 / (a * d - b * b)
             p, q, r = d * inverse, b * inverse, a * inverse
+            ratio = b / a
+            if k < 6:
+                x0, x1, y0, y1 = down(own[k], k + 2), down(own[k + 1], k + 2), down(own[k], k + 3), down(own[k + 1], k + 3)
+                xd, yd = x0 * d - x1 * b, y0 * d - y1 * b
+                xa, ya = x1 * a - x0 * b, y1 * a - y0 * b
+                a, b, d = (
+                    down(own[k + 2], k + 2) - (x0 * xd + x1 * xa) * inverse,
+                    down(own[k + 3], k + 2) - (x0 * yd + x1 * ya) * inverse,
+                    down(own[k + 3], k + 3) - (y0 * yd + y1 * ya) * inverse,
+                )
             rows = down(current, k), down(current, k + 1)
             f1 = jnp.where(below > k + 1, own[k] * p - own[k + 1] * q, 0.0)
             f2 = jnp.where(below > k + 1, own[k + 1] * r - own[k] * q, 0.0)
             for j in range(k + 2, 8):
                 own[j] = own[j] - f1 * first[j] - f2 * second[j]
-            f1 = jnp.where(below == k + 1, b / a, f1)
+            f1 = jnp.where(below == k + 1, ratio, f1)
             current = current - f1 * rows[0] - f2 * rows[1]
-            pairs.append((p, q, r, rows, first, second))
-        blocks[kb] = current
-        for b in range(kb + 1, len(blocks)):
-            columns = [across(blocks[b], 8 * kb + c) for c in range(8)]
-            for i, (p, q, r, rows, first, second) in enumerate(pairs):
-                k = 2 * i
+            for n, columns in under.items():
                 f1 = columns[k] * p - columns[k + 1] * q
                 f2 = columns[k + 1] * r - columns[k] * q
                 for j in range(k + 2, 8):
                     columns[j] = columns[j] - f1 * first[j] - f2 * second[j]
-                blocks[b] = blocks[b] - f1 * rows[0] - f2 * rows[1]
+                if n == kb + 1:
+                    for c in range(8):
+                        ahead[c] = ahead[c] - f1 * down(columns[k], c) - f2 * down(columns[k + 1], c)
+                blocks[n] = blocks[n] - f1 * rows[0] - f2 * rows[1]
+        blocks[kb] = current
+        own = ahead
     return blocks
 
 
@@ -117,7 +131,7 @@
 def kernel(
     sizes, x_hbm, s_hbm, v_hbm, d_hbm, x_out, s_out, v_out, x_ref, s_ref, v_ref, d_ref,
     k_s, base_s, tpx_s, tmx_s, t_s, k1_s, h_s, khx_s, khy_s, v_s, yface_s,
-    xhalo_s, yhalo_s, pay_s, r1_s, c_s, r2_s, f_s, r3_s, den_s, g3_s, kk_s, hh_s,
+    xhalo_s, yhalo_s, pay_s, r1_s, c_s, r2_s, f_s, r3_s, den_s, g3_s, kk_s, hh_s, v3_s,
     isem, hsend, hrecv, asend, arecv,
 ):
     ngx, ngy, slabs, ylen, zlen = sizes
@@ -282,6 +296,21 @@
     def column(row):
         return jnp.sum(eye * row, axis=1, keepdims=True)
 
+    half_lane = lax.broadcasted_iota(jnp.int32, (3 * rank, 128), 1) < rank
+
+    def doubled(a):
+        hi, lo = split(a)
+        return jnp.concatenate([hi, lo[:, :rank]], axis=1)
+
+    def pair_left(first, a):
+        turned = pltpu.roll(a, rank, 1)
+        return jnp.concatenate(
+            [doubled(first), doubled(jnp.where(half_lane, a, turned)), doubled(jnp.where(half_lane, turned, a))], axis=0
+        )
+
+    def place(j):
+        return block(1 + j // 2 + 3 * (j % 2))
+
     def flux(k, u_col):
         density = jnp.sum(k * u_col, axis=0, keepdims=True)
         return density, speed_of(density) * k
@@ -316,7 +345,7 @@
     inputs[slabs + 2].wait()
     tables, u_row = tables_of(v_ref)
     u_col = column(u_row)
-    weights = tables
+    wide = None
     prepare(u_col)
     k_left = None
     v_now = v_ref
@@ -324,18 +353,22 @@
 
     for step in range(STEPS):
         last_step = step == STEPS - 1
-        center = weights[block(0)] + weights[block(1)] + weights[block(2)]
-        center = center + weights[block(3)] + weights[block(4)] + weights[block(5)]
-        stencil = left3(c * jnp.concatenate([center, weights], axis=0))
+        if step == 0:
+            center = sum(tables[block(i)] for i in range(1, 6)) + tables[block(0)]
+            stencil = left3(c * jnp.concatenate([center] + [tables[block(i)] for i in (0, 2, 4, 1, 3, 5)], axis=0))
+        else:
+            center = wide[:, :128] + wide[:, 128:256] + wide[:, 256:]
+            weights = jnp.concatenate([wide[:, 128 * i : 128 * i + 128] for i in range(3)], axis=0)
+            stencil = pair_left(c * (center + pltpu.roll(center, rank, 1)), c * weights)
         bx = nloc
         by = nloc + 2 * slab
 
         def halo_terms():
-            tpx_s[:, :slab] = bdot(stencil[block(1)], g3_s[:, bx : bx + slab])
-            tmx_s[:, slab * slabs :] = bdot(stencil[block(3)], g3_s[:, bx + slab : bx + 2 * slab])
+            tpx_s[:, :slab] = bdot(stencil[place(0)], g3_s[:, bx : bx + slab])
+            tmx_s[:, slab * slabs :] = bdot(stencil[place(2)], g3_s[:, bx + slab : bx + 2 * slab])
             return (
-                bdot(stencil[block(2)], g3_s[:, by : by + 128]),
-                bdot(stencil[block(4)], g3_s[:, by + 128 : by + 256]),
+                bdot(stencil[place(1)], g3_s[:, by : by + 128]),
+                bdot(stencil[place(3)], g3_s[:, by + 128 : by + 256]),
             )
 
         halo = halo_copies(k1_s, step + 1)
@@ -346,12 +379,12 @@
                 k = bdot(k_left, right3(k))
             out = bdot(stencil, g3_s[:, at(q)])
             base_s[:, at(q)] = (1.0 - t) * k + t * u_col * den_s[:, at(q)] - out[:rank]
-            tpx_s[:, at(q + 1)] = out[block(1)]
-            t_s[0, :, at(q)] = out[block(2)]
-            tmx_s[:, at(q)] = out[block(3)]
-            t_s[1, :, at(q)] = out[block(4)]
-            t_s[2, :, at(q)] = out[block(5)]
-            t_s[3, :, at(q)] = out[block(6)]
+            tpx_s[:, at(q + 1)] = out[place(0)]
+            t_s[0, :, at(q)] = out[place(1)]
+            tmx_s[:, at(q)] = out[place(2)]
+            t_s[1, :, at(q)] = out[place(3)]
+            t_s[2, :, at(q)] = out[place(4)]
+            t_s[3, :, at(q)] = out[place(5)]
 
         def combine(q):
             k1_s[:, at(q)] = (
@@ -454,6 +487,9 @@
             jnp.concatenate([h_k1 - sums["x-"], h_k1 - sums["y-"], sums["x+"] - h_k1, sums["y+"] - h_k1], axis=0),
         )
         start_phase(second, 0)
+        for i in range(no // 512):
+            here = slice(512 * i, 512 * i + 512)
+            v3_s[:, here] = right3(v_now[:, here])
         for phase in range(2):
             for a in (first, second):
                 end_phase(a, phase)
@@ -461,18 +497,25 @@
         end_phase(first, 2)
         total = unpack(first)
         upper, inverse = finish(advance(begin(total[:rank]), 0, rank // 8))
-        inverse_t = mm(eye, inverse, NT)
+        none = jnp.zeros((rank, rank), F32)
+
+        def twice(a):
+            return jnp.concatenate(
+                [jnp.concatenate([a, none], axis=1), jnp.concatenate([none, a], axis=1)], axis=0
+            )
+
+        inverse_2, inverse_t = split(twice(inverse)), split(twice(mm(eye, inverse, NT)))
         q_z = mm3(inverse, total[rank : 3 * rank], NT)
+        m_z = dot3(split(q_z), inverse_t)
         signed = jnp.concatenate([tables[: 2 * rank], -tables[2 * rank : 4 * rank], tables[block(4)], -tables[block(5)]], axis=0)
+        signed = jnp.concatenate([signed, signed], axis=1)
         s_start = (1.0 + t) * upper - t * (jnp.sum(upper * u_row, axis=1, keepdims=True) * u_row)
-        s_start = s_start + c * mm3(q_z, signed[4 * rank :])
-        left = left3(inverse)
-        for q in range(slabs):
-            x1 = bdot(left, right3(k1_s[:, at(q)]))
-            if last_step:
-                x_out[at(q), :] = jnp.concatenate([x1, x1], axis=0).T[:, :rank]
-            else:
-                k_s[:, at(q)] = x1
+        s_start = jnp.concatenate([s_start, s_start], axis=1) + c * mm3(q_z, signed[4 * rank :])
+        signed = split(c * signed[: 4 * rank])
+        left = left_x = left3(inverse)
+        if not last_step:
+            for q in range(slabs):
+                k_s[:, at(q)] = bdot(left, right3(k1_s[:, at(q)]))
         if not last_step:
             halo[4].wait()
             halo[5].wait()
@@ -480,27 +523,31 @@
                 khx_s[i] = bdot(left, right3(xhalo_s[step + 1, i]))
                 khy_s[i] = bdot(left, right3(yhalo_s[step + 1, i]))
         end_phase(second, 2)
-        q_xy = mm3(inverse, unpack(second), NT)
-        s2 = s_start + c * mm3(q_xy, signed[: 4 * rank])
-        wide = jnp.concatenate([q_xy, q_z], axis=1)
-        q_stack = jnp.concatenate([wide[:, block(i)] for i in range(6)], axis=0)
-        ms2 = mm3(q_stack, mm3(inverse_t, s2))
-        mean = jnp.sum(s2 * u_row, axis=1, keepdims=True)
-        left = left3(jnp.concatenate([(1.0 - t) * s2, c * ms2], axis=0))
+        both = split(dot3(inverse_2, split(r3_s[second].reshape(128, 128) * (1.0 / cells)), NT))
+        m_all = jnp.concatenate([dot3(both, inverse_t), m_z], axis=0)
+        s2 = s_start + dot3([x[:rank] for x in both], [x[: 2 * rank] for x in signed])
+        s2 = s2 + dot3([x[rank:] for x in both], [x[2 * rank :] for x in signed])
+        s2_2 = jnp.concatenate([jnp.where(half_lane[:rank], s2, 0.0), jnp.where(half_lane[:rank], 0.0, s2)], axis=0)
+        ms2 = mm3(m_all, s2_2)
+        mean = jnp.sum(s2[:, :rank] * u_row, axis=1, keepdims=True)
+        left = pair_left((1.0 - t) * s2, c * ms2)
         gram = jnp.zeros((rank, rank), F32)
         for i in range(no // 512):
             here = slice(512 * i, 512 * i + 512)
-            out = bdot(left, right3(v_now[:, here]))
+            out = bdot(left, v3_s[:, here])
             d = d_ref[:, here]
             l1 = out[:rank] + t * mean
             for j, (dim, sign) in enumerate(signs):
-                l1 = l1 - (sign * jnp.maximum(sign * d[dim : dim + 1], 0.0)) * out[block(j + 1)]
+                l1 = l1 - (sign * jnp.maximum(sign * d[dim : dim + 1], 0.0)) * out[place(j)]
             v_s[:, here] = l1
             hi, lo = split(l1)
             gram = gram + gram3(hi, lo, hi, lo)
         v_now = v_s
         v_upper, v_inverse = finish(advance(begin(gram * (1.0 / no)), 0, rank // 8))
         if last_step:
+            for q in range(slabs):
+                x1 = bdot(left_x, right3(k1_s[:, at(q)]))
+                x_out[at(q), :] = jnp.concatenate([x1, x1], axis=0).T[:, :rank]
             left = left3(v_inverse)
             for i in range(no // 512):
                 here = slice(512 * i, 512 * i + 512)
@@ -508,21 +555,21 @@
             s_out[...] = mm(eye, v_upper, NT)
         else:
             raw_tables, raw_row = tables_of(v_s)
+            table_parts = split(raw_tables)
             raw_col = column(raw_row)
             prepare(raw_col)
             prepare_halo(raw_col)
             left = left3(v_inverse)
-            wide = mm(v_inverse, raw_tables, NT)
-            weights = jnp.concatenate([wide[:, block(i)] for i in range(6)], axis=0)
+            wide = dot3(split(v_inverse), table_parts, NT)
             u_col = jnp.sum(v_inverse * raw_row, axis=1, keepdims=True)
             u_row = jnp.sum(eye * u_col, axis=0, keepdims=True)
             k_left = left3(v_upper)
 
-            def later(left=left, weights=weights, v_inverse=v_inverse):
+            def later(left=left, wide=wide, v_inverse=v_inverse):
                 for i in range(no // 512):
                     here = slice(512 * i, 512 * i + 512)
                     v_s[:, here] = bdot(left, right3(v_s[:, here]))
-                return mm(weights, v_inverse, NT)
+                return mm(jnp.concatenate([wide[:, block(i)] for i in range(6)], axis=0), v_inverse, NT)
 
     def drain(a, _):
         for phase in range(3):
@@ -577,6 +624,7 @@
                 pltpu.VMEM((3 * rank, nloc + 2 * slab + 256), BF16),
                 pltpu.VMEM((2, rank, nloc), BF16),
                 pltpu.VMEM((2, rank, nloc), BF16),
+                pltpu.VMEM((3 * rank, no), BF16),
                 pltpu.SemaphoreType.DMA((slabs + 3,)),
                 pltpu.SemaphoreType.DMA((STEPS + 1, 6)),
                 pltpu.SemaphoreType.DMA((STEPS + 1, 6)),

time: 68.7 us -> 67.4 us (0.981)
  Pallas kernels: 67.8 us -> 66.5 us
    pallas_call x1, Pallas kernels: 66.7 us -> 65.4 us  [shards(): pl.pallas_call(functools.partial(kernel, (ngx, ngy, slabs, ylen, zlen)),...]
where the time goes in v4:
time: 67.4 us; the launch traced here: 67.3 us
  Pallas kernels  66.5 us (99%)
  between operations  0.8 us (1%)
    pallas_call x1, Pallas kernels, shards(): pl.pallas_call(functools.partial(kernel, (ngx, ngy, slabs, ylen, zlen)),...  65.4 us

profile of v4, /device:TPU:1, one launch (start us, length us, event | category | flops | bytes accessed | tf_op | source)
XLA Modules:
  0.0 67.3 jit_solution(5141578524174477369)
XLA Ops:
  0.6 65.4 %shard_map.67 = (f32[2048,64]{1,0:T(8,128)S(1)}, f32[64,64]{1,0:T(8,128)S(1)}, f32[64,2048]{1,0:T(8,128)S(1)}) custom-call(f32[2048,64]{1,0:T(8,128)} %bitcast.4, f32[64,64]{1,0:T(8,128)} %s_hbm.1, f32[64,2048]{1,0:T(8,128)} %bitcast.5, f32[3,2048]{1,0:T(4,128)} %d_hbm.1), custom_call_target="tpu_custom_call" | custom-call | tf_op jit(solution)/shard_map/pallas_call | solution.py:617
  66.0 1.2 %shard_map.68 = (f32[2048,64]{1,0:T(8,128)}, f32[64,64]{1,0:T(8,128)}, f32[64,2048]{1,0:T(8,128)}) custom-call(f32[2048,64]{1,0:T(8,128)S(1)} %get-tuple-element.9.x_ref, f32[64,64]{1,0:T(8,128)S(1)} %get-tuple-element.10.s_ref, f32[64,2048]{1,0:T(8,128)S(1)} %get-tuple-element.11.v_ref), custom_call_target="tpu_custom_call" | custom-call | tf_op jit(solution)/shard_map/pallas_call | solution.py:638

commit v5 on v4

--- a/solution.py
+++ b/solution.py
@@ -321,11 +321,23 @@
             den_s[:, at(q)] = density
             g3_s[:, at(q)] = right3(g)
 
+    half = slab // 2
+    low, high = slice(0, half), slice(half, slab)
+
+    def prepare_x(i, part, u_col):
+        here = slice(nloc + slab * i + part.start, nloc + slab * i + part.stop)
+        g3_s[:, here] = right3(flux(khx_s[i, :, part], u_col)[1])
+
+    def prepare_y(u_col):
+        for i in range(2):
+            at_y = nloc + 2 * slab + 128 * i
+            g3_s[:, at_y : at_y + 128] = right3(flux(khy_s[i], u_col)[1])
+
     def prepare_halo(u_col):
         for i in range(2):
-            g3_s[:, nloc + slab * i : nloc + slab * (i + 1)] = right3(flux(khx_s[i], u_col)[1])
-            at_y = nloc + 2 * slab + 128 * i
-            g3_s[:, at_y : at_y + 128] = right3(flux(khy_s[i], u_col)[1])
+            for part in (low, high):
+                prepare_x(i, part, u_col)
+        prepare_y(u_col)
 
     inputs[0].wait()
     st = left3(mm(eye, s_ref[...], NT))
@@ -336,7 +348,7 @@
         k_s[:, at(q)] = bdot(st[:, :rank], x_hi, NT) + bdot(st[:, rank : 2 * rank], x_lo, NT) + bdot(st[:, 2 * rank :], x_hi, NT)
         if i == 1:
             pl.semaphore_wait(barrier, ngx + ngy - 2)
-            for n in (0, 1, 4, 5):
+            for n in (4, 5, 0, 1):
                 first_halo[n].start()
     faces(k_s, 0)
     first_halo[2].start()
@@ -363,9 +375,12 @@
         bx = nloc
         by = nloc + 2 * slab
 
-        def halo_terms():
-            tpx_s[:, :slab] = bdot(stencil[place(0)], g3_s[:, bx : bx + slab])
-            tmx_s[:, slab * slabs :] = bdot(stencil[place(2)], g3_s[:, bx + slab : bx + 2 * slab])
+        def x_terms(i, part):
+            here = slice(bx + slab * i + part.start, bx + slab * i + part.stop)
+            there = slice(slab * slabs * i + part.start, slab * slabs * i + part.stop)
+            (tpx_s, tmx_s)[i][:, there] = bdot(stencil[place(2 * i)], g3_s[:, here])
+
+        def y_terms():
             return (
                 bdot(stencil[place(1)], g3_s[:, by : by + 128]),
                 bdot(stencil[place(3)], g3_s[:, by + 128 : by + 256]),
@@ -386,40 +401,67 @@
             t_s[2, :, at(q)] = out[place(4)]
             t_s[3, :, at(q)] = out[place(5)]
 
-        def combine(q):
-            k1_s[:, at(q)] = (
-                base_s[:, at(q)]
-                + tpx_s[:, at(q)]
-                + tmx_s[:, at(q + 1)]
-                + from_y_before(t_s[0, :, at(q)], tpy, q)
-                + from_y_after(t_s[1, :, at(q)], tmy, q)
-                + from_z_before(t_s[2, :, at(q)])
-                + from_z_after(t_s[3, :, at(q)])
-            )
-
+        def combine(q, chunks):
+            for n in chunks:
+                start = slab * q + 128 * n
+                here = slice(start, start + 128)
+                back, front = t_s[0, :, here], t_s[1, :, here]
+                before = roll(t_s[0, :, start - 128 : start], zlen) if n > 0 else roll(tpy, -zlen * q)
+                if n < slab // 128 - 1:
+                    after = roll(t_s[1, :, start + 128 : start + 256], -zlen)
+                else:
+                    after = roll(tmy, 128 - zlen - zlen * q)
+                k1_s[:, here] = (
+                    base_s[:, here]
+                    + tpx_s[:, here]
+                    + tmx_s[:, start + slab : start + slab + 128]
+                    + jnp.where(lane < zlen, before, roll(back, zlen))
+                    + jnp.where(lane < 128 - zlen, roll(front, -zlen), after)
+                    + from_z_before(t_s[2, :, here])
+                    + from_z_after(t_s[3, :, here])
+                )
+
+        ends = slabs - 1
+        lows, highs = range(half // 128), range(half // 128, slab // 128)
         if step == 0:
             for q in order:
                 spread(q)
-            for copy in first_halo:
-                copy.wait()
+            for n in (4, 5, 2, 3):
+                first_halo[n].wait()
+            for i, part in ((0, high), (1, low)):
+                khx_s[i, :, part] = xhalo_s[0, i, :, part]
+                khy_s[i] = yhalo_s[0, i]
+                prepare_x(i, part, u_col)
+                x_terms(i, part)
+            prepare_y(u_col)
+            tpy, tmy = y_terms()
+            combine(0, highs)
+            halo[0].start()
+            combine(ends, lows)
+            halo[1].start()
+            for n in (0, 1):
+                first_halo[n].wait()
+            for i, part in ((0, low), (1, high)):
+                khx_s[i, :, part] = xhalo_s[0, i, :, part]
+                prepare_x(i, part, u_col)
+                x_terms(i, part)
+        else:
             for i in range(2):
-                khx_s[i] = xhalo_s[0, i]
-                khy_s[i] = yhalo_s[0, i]
-            prepare_halo(u_col)
-            tpy, tmy = halo_terms()
-        else:
-            tpy, tmy = halo_terms()
+                for part in (low, high):
+                    x_terms(i, part)
+            tpy, tmy = y_terms()
             spread(0)
             spread(1)
-        combine(0)
-        halo[0].start()
-        if step > 0:
-            for q in range(slabs - 1, 1, -1):
+            combine(0, highs)
+            halo[0].start()
+            for q in range(ends, 1, -1):
                 spread(q)
-        combine(slabs - 1)
-        halo[1].start()
-        for q in range(1, slabs - 1):
-            combine(q)
+            combine(ends, lows)
+            halo[1].start()
+        combine(0, lows)
+        combine(ends, highs)
+        for q in range(1, ends):
+            combine(q, range(slab // 128))
         faces(k1_s, step + 1)
         halo[2].start()
         halo[3].start()
@@ -457,8 +499,6 @@
             for i, name in enumerate(names):
                 sums[name] = sums[name] + out[block(i)]
         y_first, y_last = split(yface_s[step + 1, 0]), split(yface_s[step + 1, 1])
-        half = slab // 2
-        low, high = slice(0, half), slice(half, slab)
         own_low, own_high = slice(0, half), slice(nloc - half, nloc)
         for copy in halo[:4]:
             copy.wait()

time: 67.4 us -> 66.7 us (0.990)
  Pallas kernels: 66.5 us -> 65.8 us
    pallas_call x1, Pallas kernels: 65.4 us -> 64.7 us  [shards(): pl.pallas_call(functools.partial(kernel, (ngx, ngy, slabs, ylen, zlen)),...]
where the time goes in v5:
time: 66.7 us; the launch traced here: 66.6 us
  Pallas kernels  65.8 us (99%)
  between operations  0.8 us (1%)
    pallas_call x1, Pallas kernels, shards(): pl.pallas_call(functools.partial(kernel, (ngx, ngy, slabs, ylen, zlen)),...  64.7 us

profile of v5, /device:TPU:1, one launch (start us, length us, event | category | flops | bytes accessed | tf_op | source)
XLA Modules:
  0.0 66.6 jit_solution(12280816104163614199)
XLA Ops:
  0.6 64.7 %shard_map.67 = (f32[2048,64]{1,0:T(8,128)S(1)}, f32[64,64]{1,0:T(8,128)S(1)}, f32[64,2048]{1,0:T(8,128)S(1)}) custom-call(f32[2048,64]{1,0:T(8,128)} %bitcast.4, f32[64,64]{1,0:T(8,128)} %s_hbm.1, f32[64,2048]{1,0:T(8,128)} %bitcast.5, f32[3,2048]{1,0:T(4,128)} %d_hbm.1), custom_call_target="tpu_custom_call" | custom-call | tf_op jit(solution)/shard_map/pallas_call | solution.py:657
  65.3 1.2 %shard_map.68 = (f32[2048,64]{1,0:T(8,128)}, f32[64,64]{1,0:T(8,128)}, f32[64,2048]{1,0:T(8,128)}) custom-call(f32[2048,64]{1,0:T(8,128)S(1)} %get-tuple-element.9.x_ref, f32[64,64]{1,0:T(8,128)S(1)} %get-tuple-element.10.s_ref, f32[64,2048]{1,0:T(8,128)S(1)} %get-tuple-element.11.v_ref), custom_call_target="tpu_custom_call" | custom-call | tf_op jit(solution)/shard_map/pallas_call | solution.py:678

commit v6 on v5

--- a/solution.py
+++ b/solution.py
@@ -458,13 +458,18 @@
                 spread(q)
             combine(ends, lows)
             halo[1].start()
-        combine(0, lows)
-        combine(ends, highs)
+        tail = slab // 128 - 1
+        combine(0, (0,))
+        combine(ends, (tail,))
         for q in range(1, ends):
-            combine(q, range(slab // 128))
+            combine(q, (0, tail))
         faces(k1_s, step + 1)
         halo[2].start()
         halo[3].start()
+        combine(0, lows[1:])
+        combine(ends, highs[:-1])
+        for q in range(1, ends):
+            combine(q, range(1, tail))
 
         first, second = 2 * step, 2 * step + 1
         raw = jnp.zeros((4 * rank, rank), F32)
@@ -478,9 +483,6 @@
             raw = raw + gram3(l_hi, l_lo, l_hi[:rank], l_lo[:rank])
         pack(first, raw)
         start_phase(first, 0)
-        if not last_step:
-            halo[4].start()
-            halo[5].start()
         h_k1 = raw[3 * rank :]
         if later is not None:
             tables = later()
@@ -527,6 +529,9 @@
             jnp.concatenate([h_k1 - sums["x-"], h_k1 - sums["y-"], sums["x+"] - h_k1, sums["y+"] - h_k1], axis=0),
         )
         start_phase(second, 0)
+        if not last_step:
+            halo[4].start()
+            halo[5].start()
         for i in range(no // 512):
             here = slice(512 * i, 512 * i + 512)
             v3_s[:, here] = right3(v_now[:, here])

time: 66.7 us -> 66.7 us (level)
  no operation moved by 1% of the time
where the time goes in v6:
time: 66.7 us; the launch traced here: 66.6 us
  Pallas kernels  65.8 us (99%)
  between operations  0.8 us (1%)
    pallas_call x1, Pallas kernels, shards(): pl.pallas_call(functools.partial(kernel, (ngx, ngy, slabs, ylen, zlen)),...  64.6 us

profile of v6, /device:TPU:1, one launch (start us, length us, event | category | flops | bytes accessed | tf_op | source)
XLA Modules:
  0.0 66.6 jit_solution(13060089263287005704)
XLA Ops:
  0.6 64.6 %shard_map.67 = (f32[2048,64]{1,0:T(8,128)S(1)}, f32[64,64]{1,0:T(8,128)S(1)}, f32[64,2048]{1,0:T(8,128)S(1)}) custom-call(f32[2048,64]{1,0:T(8,128)} %bitcast.4, f32[64,64]{1,0:T(8,128)} %s_hbm.1, f32[64,2048]{1,0:T(8,128)} %bitcast.5, f32[3,2048]{1,0:T(4,128)} %d_hbm.1), custom_call_target="tpu_custom_call" | custom-call | tf_op jit(solution)/shard_map/pallas_call | solution.py:662
  65.3 1.2 %shard_map.68 = (f32[2048,64]{1,0:T(8,128)}, f32[64,64]{1,0:T(8,128)}, f32[64,2048]{1,0:T(8,128)}) custom-call(f32[2048,64]{1,0:T(8,128)S(1)} %get-tuple-element.9.x_ref, f32[64,64]{1,0:T(8,128)S(1)} %get-tuple-element.10.s_ref, f32[64,2048]{1,0:T(8,128)S(1)} %get-tuple-element.11.v_ref), custom_call_target="tpu_custom_call" | custom-call | tf_op jit(solution)/shard_map/pallas_call | solution.py:683
